TPU v7x, 32 devices: a whole 2x2x4 slice. The times are simulated.
32 devices in a mesh: group: 4 (over z), patch: 8 (over y, x, core).
Axes of the slice: x: 2, y: 2, z: 4, core: 2. Of those that a mesh axis runs over, the one named last changes fastest.
Arguments:
- volume: float32 [4096, 8, 1024], P(('group', 'patch')), may hold values from 0.02 to 18, as said below
- block_place: int32 [4096], P(('group', 'patch')), may hold values from 0 to 4095, as said below
- measured: float32 [2, 512, 384], P(None, 'patch'), may hold values from 0.5 to 5.5
- live_rays: int32 [2, 512], replicated, may hold values from 24 to 48
Outputs:
- final_volume: float32 [4096, 8, 1024], P(('group', 'patch'))
- last_residual: float32 [4, 128, 384], P('group', 'patch')
Inputs may be any that keep to these rules, and one draw needn't show every extreme that they name: block_place lists the block positions of the 64 x 64 grid in the order of a Hilbert curve over that grid, begun at a drawn point of the curve (continuing from its end to its start) and turned or mirrored by one of the grid's eight symmetries; each position appears once. `volume`: positive.
All inputs are finite; a program needn't handle non-finite values.
Results may differ from a plain program's by a relative error of at most 0.0007.
Values may be sent and summed in bfloat16 or wider, within the bound.
A program may use at most 192 MiB of HBM per device.

v0:
```python
import math

import jax
import jax.numpy as jnp
from jax import lax
from jax.sharding import PartitionSpec as P

IMG_BLK = 64
BLK_SIDE = 32
RAYS_TILE = 48
NTILE = 64
ANG_SUB = 8
SUBSETS = 2


spread = 1.5
relax = 0.9


def footprint_tiles(place, angle_value):
    cosine = jnp.cos(angle_value)
    sine_value = jnp.sin(angle_value)
    half_image = IMG_BLK * BLK_SIDE * 0.5
    half_detector = NTILE * RAYS_TILE * 0.5
    block_col = (place % IMG_BLK).astype(jnp.float32) * BLK_SIDE - half_image
    block_row = (place // IMG_BLK).astype(jnp.float32) * BLK_SIDE - half_image
    centre = (block_col + BLK_SIDE * 0.5) * cosine + (block_row + BLK_SIDE * 0.5) * sine_value
    first_tile = jnp.floor((centre + half_detector - RAYS_TILE * 0.5) / RAYS_TILE).astype(jnp.int32)
    voxel = jnp.arange(BLK_SIDE * BLK_SIDE, dtype=jnp.int32)
    offset_col = (voxel % BLK_SIDE).astype(jnp.float32) + 0.5
    offset_row = (voxel // BLK_SIDE).astype(jnp.float32) + 0.5
    along = (block_col[:, None] + offset_col[None, :]) * cosine + (
        block_row[:, None] + offset_row[None, :]
    ) * sine_value
    ray_ids = first_tile[:, None] * RAYS_TILE + jnp.arange(2 * RAYS_TILE, dtype=jnp.int32)[None, :]
    detector = ray_ids.astype(jnp.float32) + 0.5 - half_detector
    scaled = (along[:, None, :] - detector[:, :, None]) / spread
    bump = jnp.maximum(1.0 - scaled * scaled, 0.0)
    return (first_tile, (bump * bump).astype(jnp.bfloat16))


def angle_of(angle, subset):
    return jnp.asarray(math.pi * (angle * SUBSETS + subset) / (ANG_SUB * SUBSETS), jnp.float32)


def tile_rows(angle, first_tile):
    return (angle * NTILE + first_tile[:, None] + jnp.arange(2, dtype=jnp.int32)[None, :]).reshape(
        -1
    )


def forward(rounded, place, subset):
    blocks, slices = (rounded.shape[0], rounded.shape[1])
    projection = jnp.zeros((ANG_SUB * NTILE, RAYS_TILE * slices), jnp.float32)
    ray_sum = jnp.zeros((ANG_SUB * NTILE, RAYS_TILE), jnp.float32)
    col_sum = jnp.zeros((blocks, BLK_SIDE * BLK_SIDE), jnp.float32)
    for angle in range(ANG_SUB):
        first_tile, footprint = footprint_tiles(place, angle_of(angle, subset))
        row_ids = tile_rows(angle, first_tile)
        contrib = jnp.einsum("brv,bsv->brs", footprint, rounded, preferred_element_type=jnp.float32)
        projection = projection.at[row_ids].add(contrib.reshape(2 * blocks, RAYS_TILE * slices))
        ray_part = jnp.sum(footprint, axis=2, dtype=jnp.float32)
        ray_sum = ray_sum.at[row_ids].add(ray_part.reshape(2 * blocks, RAYS_TILE))
        col_sum = col_sum + jnp.sum(footprint, axis=1, dtype=jnp.float32)
    return (projection, ray_sum, col_sum)


def backward(residual_b, place, subset):
    blocks = place.shape[0]
    slices = residual_b.shape[1] // RAYS_TILE
    total = jnp.zeros((blocks, slices, BLK_SIDE * BLK_SIDE), jnp.float32)
    for angle in range(ANG_SUB):
        first_tile, footprint = footprint_tiles(place, angle_of(angle, subset))
        picked = residual_b[tile_rows(angle, first_tile)].reshape(blocks, 2 * RAYS_TILE, slices)
        total = total + jnp.einsum(
            "brv,brs->bsv", footprint, picked, preferred_element_type=jnp.float32
        )
    return total


def residual_of(projection, ray_sum, measured_rows, live_count):
    count = projection.shape[0]
    live = (jnp.arange(RAYS_TILE, dtype=jnp.int32)[None, :] < live_count[:, None]).astype(
        jnp.float32
    )
    level = projection.reshape(count, RAYS_TILE, -1) / jnp.maximum(ray_sum, 1.0)[:, :, None]
    differ = (measured_rows.reshape(count, RAYS_TILE, -1) - level) * live[:, :, None]
    return differ.reshape(count, -1)


def shards(volume, block_place, measured, live_rays):
    groups = lax.axis_size("group")
    patches = lax.axis_size("patch")
    group_index = lax.axis_index("group")
    patch_index = lax.axis_index("patch")
    all_rows = ANG_SUB * NTILE
    slab_rows = all_rows // patches
    share_rows = slab_rows // groups
    estimate = volume
    own_residual = None
    for subset in range(SUBSETS):
        rounded = estimate.astype(jnp.bfloat16)
        projection, ray_sum, col_sum = forward(rounded, block_place, subset)
        measured_slab = measured[subset]
        live_all = live_rays[subset]
        proj_slab, raysum_slab = (
            lax.psum_scatter(projection, "patch", scatter_dimension=0, tiled=True),
            lax.psum_scatter(ray_sum, "patch", scatter_dimension=0, tiled=True),
        )
        live_slab = lax.dynamic_slice_in_dim(live_all, patch_index * slab_rows, slab_rows, 0)
        proj_total, raysum_total = lax.psum((proj_slab, raysum_slab), "group")
        residual_slab = residual_of(proj_total, raysum_total, measured_slab, live_slab)
        own_residual = lax.dynamic_slice_in_dim(
            residual_slab, group_index * share_rows, share_rows, 0
        )
        slab_residual = residual_slab.astype(jnp.bfloat16)
        residual_full = lax.all_gather(slab_residual, "patch", axis=0, tiled=True)
        backprojected = backward(residual_full, block_place, subset)
        estimate = jnp.maximum(estimate + relax * backprojected / col_sum[:, None, :], 0.0)
    return (estimate, own_residual[None])


def solution(mesh):
    return jax.shard_map(
        shards,
        mesh=mesh,
        in_specs=(
            P(("group", "patch"), None, None),
            P(("group", "patch")),
            P(None, "patch", None),
            P(),
        ),
        out_specs=(P(("group", "patch"), None, None), P("group", "patch", None)),
        check_vma=False,
    )
```

profile of v0, /device:TPU:0, one launch (start us, length us, event | category | flops | bytes accessed | tf_op | source)
XLA Modules:
  0.0 1234.7 jit_solution(9759791113310668666)
XLA Ops:
  16.6 18.3 %convert_reduce_fusion = (f32[128,1024]{1,0:T(8,128)}, f32[128,96]{1,0:T(8,128)S(1)}) fusion(f32[128,96]{1,0:T(8,128)S(1)} %convert_add_fusion, f32[128,1024]{1,0:T(8,128)S(1)} %get-tuple-element.72), kind=kLoop, calls=%fused_computation.48 | loop fusion | flops 125685760 | bytes 1146880 | tf_op jit(solution)/shard_map/reduce_sum | solution.py:64
  35.7 18.1 %convert_reduce_fusion.2 = (f32[128,1024]{1,0:T(8,128)}, f32[128,96]{1,0:T(8,128)S(1)}) fusion(f32[128,96]{1,0:T(8,128)S(1)} %get-tuple-element.138, f32[128,1024]{1,0:T(8,128)S(1)} %get-tuple-element.73), kind=kLoop, calls=%fused_computation.50 | loop fusion | flops 125685760 | bytes 1146880 | tf_op jit(solution)/shard_map/reduce_sum | solution.py:64
  54.5 18.1 %convert_reduce_fusion.4 = (f32[128,1024]{1,0:T(8,128)}, f32[128,96]{1,0:T(8,128)S(1)}) fusion(f32[128,96]{1,0:T(8,128)S(1)} %get-tuple-element.139, f32[128,1024]{1,0:T(8,128)S(1)} %get-tuple-element.74), kind=kLoop, calls=%fused_computation.52 | loop fusion | flops 125685760 | bytes 1146880 | tf_op jit(solution)/shard_map/reduce_sum | solution.py:64
  74.1 18.1 %convert_reduce_fusion.8 = (f32[128,1024]{1,0:T(8,128)}, f32[128,96]{1,0:T(8,128)}) fusion(f32[128,96]{1,0:T(8,128)S(1)} %get-tuple-element.141, f32[128,1024]{1,0:T(8,128)S(1)} %get-tuple-element.75), kind=kLoop, calls=%fused_computation.56 | loop fusion | flops 125685760 | bytes 1146880 | tf_op jit(solution)/shard_map/reduce_sum | solution.py:64
  95.1 18.1 %convert_reduce_fusion.10 = (f32[128,1024]{1,0:T(8,128)}, f32[128,96]{1,0:T(8,128)}) fusion(f32[128,96]{1,0:T(8,128)S(1)} %get-tuple-element.142, f32[128,1024]{1,0:T(8,128)S(1)} %get-tuple-element.76), kind=kLoop, calls=%fused_computation.58 | loop fusion | flops 125685760 | bytes 1146880 | tf_op jit(solution)/shard_map/reduce_sum | solution.py:64
  114.7 18.9 %convert_reduce_fusion.12 = (f32[128,1024]{1,0:T(8,128)}, f32[128,96]{1,0:T(8,128)}) fusion(f32[128,96]{1,0:T(8,128)} %get-tuple-element.143, f32[128,1024]{1,0:T(8,128)S(1)} %get-tuple-element.77), kind=kLoop, calls=%fused_computation.60 | loop fusion | flops 125685760 | bytes 1146880 | tf_op jit(solution)/shard_map/reduce_sum | solution.py:64
  137.2 19.1 %convert_reduce_fusion.14 = (f32[128,1024]{1,0:T(8,128)}, f32[128,96]{1,0:T(8,128)}) fusion(f32[128,96]{1,0:T(8,128)S(1)} %get-tuple-element.144, f32[128,1024]{1,0:T(8,128)} %get-tuple-element.78), kind=kLoop, calls=%fused_computation.62 | loop fusion | flops 125685760 | bytes 1146880 | tf_op jit(solution)/shard_map/reduce_sum | solution.py:64
  157.9 19.1 %convert_reduce_fusion.6 = (f32[128,1024]{1,0:T(8,128)}, f32[128,96]{1,0:T(8,128)}) fusion(f32[128,96]{1,0:T(8,128)} %get-tuple-element.140, f32[128,1024]{1,0:T(8,128)S(1)} %get-tuple-element.86), kind=kLoop, calls=%fused_computation.54 | loop fusion | flops 125685760 | bytes 1146880 | tf_op jit(solution)/shard_map/reduce_sum | solution.py:64
  210.9 18.9 %convert_reduce_fusion.16 = (f32[128,1024]{1,0:T(8,128)}, f32[128,96]{1,0:T(8,128)S(1)}) fusion(f32[128,96]{1,0:T(8,128)} %get-tuple-element.145, f32[128,1024]{1,0:T(8,128)S(1)} %copy-done.24), kind=kLoop, calls=%fused_computation.64 | loop fusion | flops 125685760 | bytes 1146880 | tf_op jit(solution)/shard_map/reduce_sum | solution.py:64
  230.7 18.1 %convert_reduce_fusion.20 = (f32[128,1024]{1,0:T(8,128)}, f32[128,96]{1,0:T(8,128)S(1)}) fusion(f32[128,96]{1,0:T(8,128)S(1)} %get-tuple-element.147, f32[128,1024]{1,0:T(8,128)S(1)} %copy-done.27), kind=kLoop, calls=%fused_computation.68 | loop fusion | flops 125685760 | bytes 1146880 | tf_op jit(solution)/shard_map/reduce_sum | solution.py:64
  251.4 18.1 %convert_reduce_fusion.22 = (f32[128,1024]{1,0:T(8,128)}, f32[128,96]{1,0:T(8,128)S(1)}) fusion(f32[128,96]{1,0:T(8,128)S(1)} %get-tuple-element.148, f32[128,1024]{1,0:T(8,128)S(1)} %copy-done.28), kind=kLoop, calls=%fused_computation.70 | loop fusion | flops 125685760 | bytes 1146880 | tf_op jit(solution)/shard_map/reduce_sum | solution.py:64
  270.2 18.9 %convert_reduce_fusion.24 = (f32[128,1024]{1,0:T(8,128)}, f32[128,96]{1,0:T(8,128)S(1)}) fusion(f32[128,96]{1,0:T(8,128)} %get-tuple-element.149, f32[128,1024]{1,0:T(8,128)S(1)} %copy-done.29), kind=kLoop, calls=%fused_computation.72 | loop fusion | flops 125685760 | bytes 1146880 | tf_op jit(solution)/shard_map/reduce_sum | solution.py:64
  291.2 18.1 %convert_reduce_fusion.26 = (f32[128,1024]{1,0:T(8,128)}, f32[128,96]{1,0:T(8,128)S(1)}) fusion(f32[128,96]{1,0:T(8,128)S(1)} %get-tuple-element.150, f32[128,1024]{1,0:T(8,128)S(1)} %copy-done.30), kind=kLoop, calls=%fused_computation.74 | loop fusion | flops 125685760 | bytes 1146880 | tf_op jit(solution)/shard_map/reduce_sum | solution.py:64
  309.4 19.3 %convert_reduce_fusion.28 = (f32[128,1024]{1,0:T(8,128)}, f32[128,96]{1,0:T(8,128)S(1)}) fusion(f32[128,96]{1,0:T(8,128)} %get-tuple-element.151, f32[128,1024]{1,0:T(8,128)} %get-tuple-element.84), kind=kLoop, calls=%fused_computation.76 | loop fusion | flops 125685760 | bytes 1146880 | tf_op jit(solution)/shard_map/reduce_sum | solution.py:64
  329.4 18.1 %convert_reduce_fusion.18 = (f32[128,1024]{1,0:T(8,128)}, f32[128,96]{1,0:T(8,128)S(1)}) fusion(f32[128,96]{1,0:T(8,128)S(1)} %get-tuple-element.146, f32[128,1024]{1,0:T(8,128)S(1)} %copy-done.25), kind=kLoop, calls=%fused_computation.66 | loop fusion | flops 125685760 | bytes 1146880 | tf_op jit(solution)/shard_map/reduce_sum | solution.py:64
  347.6 19.3 %convert_reduce_fusion.30 = (f32[128,1024]{1,0:T(8,128)}, f32[128,96]{1,0:T(8,128)S(1)}) fusion(f32[128,96]{1,0:T(8,128)S(1)} %convert_add_fusion.15, f32[128,1024]{1,0:T(8,128)} %get-tuple-element.87), kind=kLoop, calls=%fused_computation.78 | loop fusion | flops 125685760 | bytes 1146880 | tf_op jit(solution)/shard_map/reduce_sum | solution.py:64
  389.2 13.4 %fusion.15 = f32[128,96,8]{2,1,0:T(8,128)} fusion(bf16[128,8,1024]{2,1,0:T(8,128)(2,1)S(1)} %convert_element_type.235, f32[128,96]{1,0:T(8,128)S(1)} %copy-done.62, f32[128,1024]{1,0:T(8,128)S(1)} %copy-done.24), kind=kOutput, calls=%fused_computation.111 | convolution fusion | flops 289406976 | bytes 3063808 | tf_op jit(solution)/shard_map/brv,bsv->brs/dot_general | solution.py:60
  402.6 13.2 %fusion.11 = f32[128,96,8]{2,1,0:T(8,128)} fusion(bf16[128,8,1024]{2,1,0:T(8,128)(2,1)S(1)} %convert_element_type.235, f32[128,96]{1,0:T(8,128)S(1)} %copy-done.68, f32[128,1024]{1,0:T(8,128)S(1)} %copy-done.27), kind=kOutput, calls=%fused_computation.107 | convolution fusion | flops 289406976 | bytes 3063808 | tf_op jit(solution)/shard_map/brv,bsv->brs/dot_general | solution.py:60
  442.2 13.3 %fusion.5 = f32[128,96,8]{2,1,0:T(8,128)} fusion(bf16[128,8,1024]{2,1,0:T(8,128)(2,1)S(1)} %convert_element_type.235, f32[128,96]{1,0:T(8,128)S(1)} %copy-done.76, f32[128,1024]{1,0:T(8,128)S(1)} %copy-done.31), kind=kOutput, calls=%fused_computation.101 | convolution fusion | flops 289406976 | bytes 3063808 | tf_op jit(solution)/shard_map/brv,bsv->brs/dot_general | solution.py:60
  455.5 13.2 %fusion.3 = f32[128,96,8]{2,1,0:T(8,128)} fusion(bf16[128,8,1024]{2,1,0:T(8,128)(2,1)S(1)} %convert_element_type.235, f32[128,96]{1,0:T(8,128)S(1)} %copy-done.77, f32[128,1024]{1,0:T(8,128)S(1)} %copy-done.32), kind=kOutput, calls=%fused_computation.99 | convolution fusion | flops 289406976 | bytes 3063808 | tf_op jit(solution)/shard_map/brv,bsv->brs/dot_general | solution.py:60
  468.8 13.3 %fusion.13 = f32[128,96,8]{2,1,0:T(8,128)} fusion(bf16[128,8,1024]{2,1,0:T(8,128)(2,1)S(1)} %convert_element_type.235, f32[128,96]{1,0:T(8,128)S(1)} %copy-done.65, f32[128,1024]{1,0:T(8,128)S(1)} %copy-done.26), kind=kOutput, calls=%fused_computation.109 | convolution fusion | flops 289406976 | bytes 3063808 | tf_op jit(solution)/shard_map/brv,bsv->brs/dot_general | solution.py:60
  482.0 13.3 %fusion.1 = f32[128,96,8]{2,1,0:T(8,128)} fusion(bf16[128,8,1024]{2,1,0:T(8,128)(2,1)S(1)} %convert_element_type.235, f32[128,96]{1,0:T(8,128)S(1)} %copy-done.71, f32[128,1024]{1,0:T(8,128)S(1)} %copy-done.33), kind=kOutput, calls=%fused_computation.97 | convolution fusion | flops 289406976 | bytes 3063808 | tf_op jit(solution)/shard_map/brv,bsv->brs/dot_general | solution.py:60
  566.9 22.0 %all-reduce = (f32[64,48]{0,1:T(8,128)S(1)}, f32[64,48]{0,1:T(8,128)}) all-reduce(f32[64,48]{0,1:T(8,128)S(1)} %copy.205, f32[64,48]{0,1:T(8,128)S(1)} %copy.207), channel_id=1, replica_groups=mesh['group'=4,'patch'=8] {'group'}, use_global_device_ids=true, to_apply=%region_27.28 | all-reduce | flops 6144 | bytes 49152 | tf_op jit(solution)/shard_map/psum | solution.py:111
  598.4 36.5 %all-reduce.4.cloned.1.call-done = f32[64,384]{1,0:T(8,128)} async-done(((f32[64,384]{1,0:T(8,128)}), f32[64,384]{1,0:T(8,128)}) %all-reduce.4.cloned.1.call-update) | async-done | bytes 98320 | tf_op jit(solution)/shard_map/psum | solution.py:111
  663.7 14.0 %fusion = f32[128,8,1024]{2,1,0:T(8,128)} fusion(bf16[128,96,8]{2,1,0:T(8,128)(2,1)S(1)} %reshape.1902, f32[128,96]{1,0:T(8,128)} %copy-done.70, f32[128,1024]{1,0:T(8,128)} %get-tuple-element.87), kind=kOutput, calls=%fused_computation.96 | convolution fusion | flops 289406976 | bytes 4964352 | tf_op jit(solution)/shard_map/brv,brs->bsv/dot_general | solution.py:75
  682.3 14.0 %fusion.2 = f32[128,8,1024]{2,1,0:T(8,128)} fusion(bf16[128,96,8]{2,1,0:T(8,128)(2,1)S(1)} %reshape.1903, f32[128,96]{1,0:T(8,128)} %get-tuple-element.151, f32[128,1024]{1,0:T(8,128)} %get-tuple-element.84), kind=kOutput, calls=%fused_computation.98 | convolution fusion | flops 289406976 | bytes 4964352 | tf_op jit(solution)/shard_map/brv,brs->bsv/dot_general | solution.py:75
  701.0 14.0 %fusion.4 = f32[128,8,1024]{2,1,0:T(8,128)} fusion(bf16[128,96,8]{2,1,0:T(8,128)(2,1)S(1)} %reshape.1904, f32[128,96]{1,0:T(8,128)} %copy-done.75, f32[128,1024]{1,0:T(8,128)} %get-tuple-element.83), kind=kOutput, calls=%fused_computation.100 | convolution fusion | flops 289406976 | bytes 4964352 | tf_op jit(solution)/shard_map/brv,brs->bsv/dot_general | solution.py:75
  719.7 13.9 %fusion.6 = f32[128,8,1024]{2,1,0:T(8,128)} fusion(bf16[128,96,8]{2,1,0:T(8,128)(2,1)S(1)} %reshape.1905, f32[128,96]{1,0:T(8,128)} %get-tuple-element.149, f32[128,1024]{1,0:T(8,128)} %get-tuple-element.82), kind=kOutput, calls=%fused_computation.102 | convolution fusion | flops 289406976 | bytes 4964352 | tf_op jit(solution)/shard_map/brv,brs->bsv/dot_general | solution.py:75
  737.4 14.0 %fusion.8 = f32[128,8,1024]{2,1,0:T(8,128)} fusion(bf16[128,96,8]{2,1,0:T(8,128)(2,1)S(1)} %reshape.1906, f32[128,96]{1,0:T(8,128)} %copy-done.72, f32[128,1024]{1,0:T(8,128)} %get-tuple-element.81), kind=kOutput, calls=%fused_computation.104 | convolution fusion | flops 289406976 | bytes 4964352 | tf_op jit(solution)/shard_map/brv,brs->bsv/dot_general | solution.py:75
  755.0 14.0 %fusion.10 = f32[128,8,1024]{2,1,0:T(8,128)} fusion(bf16[128,96,8]{2,1,0:T(8,128)(2,1)S(1)} %reshape.1907, f32[128,96]{1,0:T(8,128)S(1)} %copy-done.69, f32[128,1024]{1,0:T(8,128)} %get-tuple-element.80), kind=kOutput, calls=%fused_computation.106 | convolution fusion | flops 289406976 | bytes 4964352 | tf_op jit(solution)/shard_map/brv,brs->bsv/dot_general | solution.py:75
  772.6 14.0 %fusion.12 = f32[128,8,1024]{2,1,0:T(8,128)} fusion(bf16[128,96,8]{2,1,0:T(8,128)(2,1)S(1)} %reshape.1908, f32[128,96]{1,0:T(8,128)S(1)} %copy-done.66, f32[128,1024]{1,0:T(8,128)} %get-tuple-element.85), kind=kOutput, calls=%fused_computation.108 | convolution fusion | flops 289406976 | bytes 4964352 | tf_op jit(solution)/shard_map/brv,brs->bsv/dot_general | solution.py:75
  790.2 19.1 %fusion.172 = (bf16[128,8,1024]{2,1,0:T(8,128)(2,1)S(1)}, f32[128,8,1024]{2,1,0:T(8,128)}) fusion(f32[128,8,1024]{2,1,0:T(8,128)} %param.4, f32[128,1024]{1,0:T(8,128)} %add_add_fusion.3, bf16[128,96,8]{2,1,0:T(8,128)(2,1)S(1)} %reshape.1909, f32[128,96]{1,0:T(8,128)S(1)} %copy-done.63, f32[128,1024]{1,0:T(8,128)} %get-tuple-element.79, ...), kind=kOutput, calls=%fused_computation.438 | convolution fusion | flops 301989888 | bytes 41140224 | tf_op jit(solution)/shard_map/brv,brs->bsv/dot_general | solution.py:75
  809.3 13.4 %fusion.31 = f32[128,96,8]{2,1,0:T(8,128)} fusion(bf16[128,8,1024]{2,1,0:T(8,128)(2,1)S(1)} %get-tuple-element.118, f32[128,96]{1,0:T(8,128)S(1)} %copy-done.46, f32[128,1024]{1,0:T(8,128)S(1)} %copy-done.5), kind=kOutput, calls=%fused_computation.127 | convolution fusion | flops 289406976 | bytes 3063808 | tf_op jit(solution)/shard_map/brv,bsv->brs/dot_general | solution.py:60
  822.8 13.3 %fusion.29 = f32[128,96,8]{2,1,0:T(8,128)} fusion(bf16[128,8,1024]{2,1,0:T(8,128)(2,1)S(1)} %get-tuple-element.118, f32[128,96]{1,0:T(8,128)S(1)} %copy-done.49, f32[128,1024]{1,0:T(8,128)S(1)} %copy-done.7), kind=kOutput, calls=%fused_computation.125 | convolution fusion | flops 289406976 | bytes 3063808 | tf_op jit(solution)/shard_map/brv,bsv->brs/dot_general | solution.py:60
  836.0 13.3 %fusion.27 = f32[128,96,8]{2,1,0:T(8,128)} fusion(bf16[128,8,1024]{2,1,0:T(8,128)(2,1)S(1)} %get-tuple-element.118, f32[128,96]{1,0:T(8,128)S(1)} %copy-done.52, f32[128,1024]{1,0:T(8,128)S(1)} %copy-done.9), kind=kOutput, calls=%fused_computation.123 | convolution fusion | flops 289406976 | bytes 3063808 | tf_op jit(solution)/shard_map/brv,bsv->brs/dot_general | solution.py:60
  849.3 13.2 %fusion.25 = f32[128,96,8]{2,1,0:T(8,128)} fusion(bf16[128,8,1024]{2,1,0:T(8,128)(2,1)S(1)} %get-tuple-element.118, f32[128,96]{1,0:T(8,128)S(1)} %copy-done.54, f32[128,1024]{1,0:T(8,128)S(1)} %copy-done.11), kind=kOutput, calls=%fused_computation.121 | convolution fusion | flops 289406976 | bytes 3063808 | tf_op jit(solution)/shard_map/brv,bsv->brs/dot_general | solution.py:60
  875.8 13.3 %fusion.21 = f32[128,96,8]{2,1,0:T(8,128)} fusion(bf16[128,8,1024]{2,1,0:T(8,128)(2,1)S(1)} %get-tuple-element.118, f32[128,96]{1,0:T(8,128)S(1)} %copy-done.58, f32[128,1024]{1,0:T(8,128)S(1)} %copy-done.15), kind=kOutput, calls=%fused_computation.117 | convolution fusion | flops 289406976 | bytes 3063808 | tf_op jit(solution)/shard_map/brv,bsv->brs/dot_general | solution.py:60
  902.3 13.2 %fusion.17 = f32[128,96,8]{2,1,0:T(8,128)} fusion(bf16[128,8,1024]{2,1,0:T(8,128)(2,1)S(1)} %get-tuple-element.118, f32[128,96]{1,0:T(8,128)S(1)} %copy-done.61, f32[128,1024]{1,0:T(8,128)S(1)} %copy-done.18), kind=kOutput, calls=%fused_computation.113 | convolution fusion | flops 289406976 | bytes 3063808 | tf_op jit(solution)/shard_map/brv,bsv->brs/dot_general | solution.py:60
  984.3 30.1 %reduce-scatter.11.cloned.1.call-done = f32[64,384]{1,0:T(8,128)} async-done(((f32[512,384]{1,0:T(8,128)}), f32[64,384]{1,0:T(8,128)}) %reduce-scatter.11.cloned.1.call-update) | async-done | bytes 98320 | tf_op jit(solution)/shard_map/reduce_scatter | solution.py:107
  1014.6 36.5 %all-reduce.6.cloned.1.call-done = f32[64,384]{1,0:T(8,128)} async-done(((f32[64,384]{1,0:T(8,128)}), f32[64,384]{1,0:T(8,128)}) %all-reduce.6.cloned.1.call-update) | async-done | bytes 98320 | tf_op jit(solution)/shard_map/psum | solution.py:111
  1080.9 14.0 %fusion.16 = f32[128,8,1024]{2,1,0:T(8,128)} fusion(bf16[128,96,8]{2,1,0:T(8,128)(2,1)S(1)} %reshape.1926, f32[128,96]{1,0:T(8,128)} %copy-done.60, f32[128,1024]{1,0:T(8,128)} %get-tuple-element.78), kind=kOutput, calls=%fused_computation.112 | convolution fusion | flops 289406976 | bytes 4964352 | tf_op jit(solution)/shard_map/brv,brs->bsv/dot_general | solution.py:75
  1099.6 14.0 %fusion.18 = f32[128,8,1024]{2,1,0:T(8,128)} fusion(bf16[128,96,8]{2,1,0:T(8,128)(2,1)S(1)} %reshape.1927, f32[128,96]{1,0:T(8,128)} %get-tuple-element.143, f32[128,1024]{1,0:T(8,128)} %copy-done.16), kind=kOutput, calls=%fused_computation.114 | convolution fusion | flops 289406976 | bytes 4964352 | tf_op jit(solution)/shard_map/brv,brs->bsv/dot_general | solution.py:75
  1118.2 14.0 %fusion.20 = f32[128,8,1024]{2,1,0:T(8,128)} fusion(bf16[128,96,8]{2,1,0:T(8,128)(2,1)S(1)} %reshape.1928, f32[128,96]{1,0:T(8,128)} %copy-done.57, f32[128,1024]{1,0:T(8,128)} %copy-done.14), kind=kOutput, calls=%fused_computation.116 | convolution fusion | flops 289406976 | bytes 4964352 | tf_op jit(solution)/shard_map/brv,brs->bsv/dot_general | solution.py:75
  1136.9 13.9 %fusion.22 = f32[128,8,1024]{2,1,0:T(8,128)} fusion(bf16[128,96,8]{2,1,0:T(8,128)(2,1)S(1)} %reshape.1929, f32[128,96]{1,0:T(8,128)} %copy-done.55, f32[128,1024]{1,0:T(8,128)} %copy-done.12), kind=kOutput, calls=%fused_computation.118 | convolution fusion | flops 289406976 | bytes 4964352 | tf_op jit(solution)/shard_map/brv,brs->bsv/dot_general | solution.py:75
  1154.6 14.0 %fusion.24 = f32[128,8,1024]{2,1,0:T(8,128)} fusion(bf16[128,96,8]{2,1,0:T(8,128)(2,1)S(1)} %reshape.1930, f32[128,96]{1,0:T(8,128)} %get-tuple-element.140, f32[128,1024]{1,0:T(8,128)} %copy-done.10), kind=kOutput, calls=%fused_computation.120 | convolution fusion | flops 289406976 | bytes 4964352 | tf_op jit(solution)/shard_map/brv,brs->bsv/dot_general | solution.py:75
  1172.3 14.0 %fusion.26 = f32[128,8,1024]{2,1,0:T(8,128)} fusion(bf16[128,96,8]{2,1,0:T(8,128)(2,1)S(1)} %reshape.1931, f32[128,96]{1,0:T(8,128)S(1)} %copy-done.53, f32[128,1024]{1,0:T(8,128)} %copy-done.8), kind=kOutput, calls=%fused_computation.122 | convolution fusion | flops 289406976 | bytes 4964352 | tf_op jit(solution)/shard_map/brv,brs->bsv/dot_general | solution.py:75
  1189.9 14.0 %fusion.28 = f32[128,8,1024]{2,1,0:T(8,128)} fusion(bf16[128,96,8]{2,1,0:T(8,128)(2,1)S(1)} %reshape.1932, f32[128,96]{1,0:T(8,128)S(1)} %copy-done.50, f32[128,1024]{1,0:T(8,128)} %copy-done.6), kind=kOutput, calls=%fused_computation.124 | convolution fusion | flops 289406976 | bytes 4964352 | tf_op jit(solution)/shard_map/brv,brs->bsv/dot_general | solution.py:75
  1208.8 18.9 %add_maximum_fusion = f32[128,8,1024]{2,1,0:T(8,128)} fusion(f32[128,8,1024]{2,1,0:T(8,128)} %get-tuple-element.119, f32[128,8,1024]{2,1,0:T(8,128)} %fusion.28, f32[128,8,1024]{2,1,0:T(8,128)} %fusion.26, f32[128,8,1024]{2,1,0:T(8,128)} %fusion.24, f32[128,8,1024]{2,1,0:T(8,128)} %fusion.22, f32[128,8,1024]{2,1,0:T(8,128)} %fusion.20, ...), kind=kOutput, calls=%fused_computation.128 | convolution fusion | flops 300941312 | bytes 39043072 | tf_op jit(solution)/shard_map/brv,brs->bsv/dot_general | solution.py:75
  (447 shorter events, 404.3 us)
Async XLA Ops:
  7.2 558.0 %reduce-scatter.15.cloned.1.call-start = ((), (), s32[]{:S(2)}) async-start(), calls=%async_computation.9 | async-start | bytes 294912
  8.8 63.8 %copy-start.45 = (f32[128,96]{1,0:T(8,128)}, f32[128,96]{1,0:T(8,128)S(1)}, u32[]{:S(2)}) copy-start(f32[128,96]{1,0:T(8,128)S(1)} %convert_add_fusion) | copy-start | bytes 147460
  15.8 165.9 %copy-start.6 = (f32[128,1024]{1,0:T(8,128)}, f32[128,1024]{1,0:T(8,128)S(1)}, u32[]{:S(2)}) copy-start(f32[128,1024]{1,0:T(8,128)S(1)} %get-tuple-element.73) | copy-start | bytes 1572868
  15.8 170.3 %copy-start.8 = (f32[128,1024]{1,0:T(8,128)}, f32[128,1024]{1,0:T(8,128)S(1)}, u32[]{:S(2)}) copy-start(f32[128,1024]{1,0:T(8,128)S(1)} %get-tuple-element.74) | copy-start | bytes 1572868
  15.8 170.3 %copy-start.10 = (f32[128,1024]{1,0:T(8,128)}, f32[128,1024]{1,0:T(8,128)S(1)}, u32[]{:S(2)}) copy-start(f32[128,1024]{1,0:T(8,128)S(1)} %get-tuple-element.86) | copy-start | bytes 1572868
  15.8 170.3 %copy-start.12 = (f32[128,1024]{1,0:T(8,128)}, f32[128,1024]{1,0:T(8,128)S(1)}, u32[]{:S(2)}) copy-start(f32[128,1024]{1,0:T(8,128)S(1)} %get-tuple-element.75) | copy-start | bytes 1572868
  15.8 170.3 %copy-start.14 = (f32[128,1024]{1,0:T(8,128)}, f32[128,1024]{1,0:T(8,128)S(1)}, u32[]{:S(2)}) copy-start(f32[128,1024]{1,0:T(8,128)S(1)} %get-tuple-element.76) | copy-start | bytes 1572868
  15.8 170.3 %copy-start.16 = (f32[128,1024]{1,0:T(8,128)}, f32[128,1024]{1,0:T(8,128)S(1)}, u32[]{:S(2)}) copy-start(f32[128,1024]{1,0:T(8,128)S(1)} %get-tuple-element.77) | copy-start | bytes 1572868
  35.7 18.8 %copy-start.48 = (f32[128,96]{1,0:T(8,128)}, f32[128,96]{1,0:T(8,128)S(1)}, u32[]{:S(2)}) copy-start(f32[128,96]{1,0:T(8,128)S(1)} %get-tuple-element.138) | copy-start | bytes 147460
  35.7 56.5 %copy-start.51 = (f32[128,96]{1,0:T(8,128)}, f32[128,96]{1,0:T(8,128)S(1)}, u32[]{:S(2)}) copy-start(f32[128,96]{1,0:T(8,128)S(1)} %get-tuple-element.139) | copy-start | bytes 147460
  74.1 18.1 %copy-start.55 = (f32[128,96]{1,0:T(8,128)}, f32[128,96]{1,0:T(8,128)S(1)}, u32[]{:S(2)}) copy-start(f32[128,96]{1,0:T(8,128)S(1)} %get-tuple-element.141) | copy-start | bytes 147460
  179.8 17.9 %copy-start.80 = (s32[256,1]{0,1:T(1,128)}, s32[256,1]{0,1:T(1,128)S(1)}, u32[]{:S(2)}) copy-start(s32[256,1]{0,1:T(1,128)S(1)} %get-tuple-element.124) | copy-start | bytes 3076
  180.4 17.3 %copy-start.84 = (s32[256,1]{0,1:T(1,128)}, s32[256,1]{0,1:T(1,128)S(1)}, u32[]{:S(2)}) copy-start(s32[256,1]{0,1:T(1,128)S(1)} %get-tuple-element.121) | copy-start | bytes 3076
  180.4 17.3 %copy-start.82 = (s32[256,1]{0,1:T(1,128)}, s32[256,1]{0,1:T(1,128)S(1)}, u32[]{:S(2)}) copy-start(s32[256,1]{0,1:T(1,128)S(1)} %get-tuple-element.120) | copy-start | bytes 3076
  181.7 16.0 %copy-start.86 = (s32[256,1]{0,1:T(1,128)}, s32[256,1]{0,1:T(1,128)S(1)}, u32[]{:S(2)}) copy-start(s32[256,1]{0,1:T(1,128)S(1)} %get-tuple-element.126) | copy-start | bytes 3076
  188.5 22.4 %copy-start.24 = (f32[128,1024]{1,0:T(8,128)S(1)}, f32[128,1024]{1,0:T(8,128)}, u32[]{:S(2)}) copy-start(f32[128,1024]{1,0:T(8,128)} %get-tuple-element.79) | copy-start | bytes 1572868
  190.6 40.0 %copy-start.27 = (f32[128,1024]{1,0:T(8,128)S(1)}, f32[128,1024]{1,0:T(8,128)}, u32[]{:S(2)}) copy-start(f32[128,1024]{1,0:T(8,128)} %get-tuple-element.80) | copy-start | bytes 1572868
  190.6 60.8 %copy-start.28 = (f32[128,1024]{1,0:T(8,128)S(1)}, f32[128,1024]{1,0:T(8,128)}, u32[]{:S(2)}) copy-start(f32[128,1024]{1,0:T(8,128)} %get-tuple-element.81) | copy-start | bytes 1572868
  193.1 77.1 %copy-start.29 = (f32[128,1024]{1,0:T(8,128)S(1)}, f32[128,1024]{1,0:T(8,128)}, u32[]{:S(2)}) copy-start(f32[128,1024]{1,0:T(8,128)} %get-tuple-element.82) | copy-start | bytes 1572868
  195.2 96.0 %copy-start.30 = (f32[128,1024]{1,0:T(8,128)S(1)}, f32[128,1024]{1,0:T(8,128)}, u32[]{:S(2)}) copy-start(f32[128,1024]{1,0:T(8,128)} %get-tuple-element.83) | copy-start | bytes 1572868
  197.7 131.7 %copy-start.25 = (f32[128,1024]{1,0:T(8,128)S(1)}, f32[128,1024]{1,0:T(8,128)}, u32[]{:S(2)}) copy-start(f32[128,1024]{1,0:T(8,128)} %get-tuple-element.85) | copy-start | bytes 1572868
  200.5 365.5 %reduce-scatter.13.cloned.1.call-start = ((), (), s32[]{:S(2)}) async-start(), calls=%async_computation.8 | async-start | bytes 294912
  209.5 159.5 %copy-start.70 = (f32[128,96]{1,0:T(8,128)}, f32[128,96]{1,0:T(8,128)S(1)}, u32[]{:S(2)}) copy-start(f32[128,96]{1,0:T(8,128)S(1)} %convert_add_fusion.15) | copy-start | bytes 147460
  230.6 138.4 %copy-start.64 = (f32[128,96]{1,0:T(8,128)}, f32[128,96]{1,0:T(8,128)S(1)}, u32[]{:S(2)}) copy-start(f32[128,96]{1,0:T(8,128)S(1)} %get-tuple-element.146) | copy-start | bytes 147460
  230.6 138.4 %copy-start.67 = (f32[128,96]{1,0:T(8,128)}, f32[128,96]{1,0:T(8,128)S(1)}, u32[]{:S(2)}) copy-start(f32[128,96]{1,0:T(8,128)S(1)} %get-tuple-element.147) | copy-start | bytes 147460
  291.2 18.1 %copy-start.75 = (f32[128,96]{1,0:T(8,128)}, f32[128,96]{1,0:T(8,128)S(1)}, u32[]{:S(2)}) copy-start(f32[128,96]{1,0:T(8,128)S(1)} %get-tuple-element.150) | copy-start | bytes 147460
  309.3 65.8 %copy-start.44 = (f32[256,48]{1,0:T(8,128)S(1)}, f32[256,48]{1,0:T(8,128)}, u32[]{:S(2)}) copy-start(f32[256,48]{1,0:T(8,128)} %reshape.2154) | copy-start | bytes 147460
  328.6 50.9 %copy-start.43 = (f32[256,48]{1,0:T(8,128)S(1)}, f32[256,48]{1,0:T(8,128)}, u32[]{:S(2)}) copy-start(f32[256,48]{1,0:T(8,128)} %reshape.2170) | copy-start | bytes 147460
  367.6 16.1 %copy-start.96 = (s32[256,1]{0,1:T(1,128)}, s32[256,1]{0,1:T(1,128)S(1)}, u32[]{:S(2)}) copy-start(s32[256,1]{0,1:T(1,128)S(1)} %get-tuple-element.130) | copy-start | bytes 3076
  367.6 16.1 %copy-start.98 = (s32[256,1]{0,1:T(1,128)}, s32[256,1]{0,1:T(1,128)S(1)}, u32[]{:S(2)}) copy-start(s32[256,1]{0,1:T(1,128)S(1)} %get-tuple-element.131) | copy-start | bytes 3076
  368.3 15.4 %copy-start.100 = (s32[256,1]{0,1:T(1,128)}, s32[256,1]{0,1:T(1,128)S(1)}, u32[]{:S(2)}) copy-start(s32[256,1]{0,1:T(1,128)S(1)} %get-tuple-element.132) | copy-start | bytes 3076
  368.3 15.4 %copy-start.102 = (s32[256,1]{0,1:T(1,128)}, s32[256,1]{0,1:T(1,128)S(1)}, u32[]{:S(2)}) copy-start(s32[256,1]{0,1:T(1,128)S(1)} %get-tuple-element.133) | copy-start | bytes 3076
  369.0 14.8 %copy-start.110 = (s32[256,1]{0,1:T(1,128)}, s32[256,1]{0,1:T(1,128)S(1)}, u32[]{:S(2)}) copy-start(s32[256,1]{0,1:T(1,128)S(1)} %get-tuple-element.135) | copy-start | bytes 3076
  381.6 21.0 %copy-start.104 = (s32[256,1]{0,1:T(1,128)}, s32[256,1]{0,1:T(1,128)S(1)}, u32[]{:S(2)}) copy-start(s32[256,1]{0,1:T(1,128)S(1)} %get-tuple-element.128) | copy-start | bytes 3076
  381.7 20.9 %copy-start.106 = (s32[256,1]{0,1:T(1,128)}, s32[256,1]{0,1:T(1,128)S(1)}, u32[]{:S(2)}) copy-start(s32[256,1]{0,1:T(1,128)S(1)} %get-tuple-element.129) | copy-start | bytes 3076
  386.6 211.6 %reduce-scatter.9.cloned.1.call-start = ((), (), s32[]{:S(2)}) async-start(), calls=%async_computation.4 | async-start | bytes 884736 | tf_op jit(solution)/shard_map/reduce_scatter | solution.py:107
  560.3 74.5 %copy-start.78 = (f32[2,64,384]{2,1,0:T(8,128)S(1)}, f32[2,64,384]{2,1,0:T(8,128)}, u32[]{:S(2)}) copy-start(f32[2,64,384]{2,1,0:T(8,128)} %param.6) | copy-start | bytes 589828
  560.3 74.5 %all-reduce.4.cloned.1.call-start = ((), (), s32[]{:S(2)}) async-start(), calls=%async_computation.5 | async-start | bytes 196608 | tf_op jit(solution)/shard_map/psum | solution.py:111
  598.2 416.3 %reduce-scatter.11.cloned.1.call-start = ((), (), s32[]{:S(2)}) async-start(), calls=%async_computation.6 | async-start | bytes 884736 | tf_op jit(solution)/shard_map/reduce_scatter | solution.py:107
  737.4 17.6 %copy-start.69 = (f32[128,96]{1,0:T(8,128)S(1)}, f32[128,96]{1,0:T(8,128)}, u32[]{:S(2)}) copy-start(f32[128,96]{1,0:T(8,128)} %copy-done.67) | copy-start | bytes 147460
  755.0 17.6 %copy-start.66 = (f32[128,96]{1,0:T(8,128)S(1)}, f32[128,96]{1,0:T(8,128)}, u32[]{:S(2)}) copy-start(f32[128,96]{1,0:T(8,128)} %copy-done.64) | copy-start | bytes 147460
  772.6 17.6 %copy-start.63 = (f32[128,96]{1,0:T(8,128)S(1)}, f32[128,96]{1,0:T(8,128)}, u32[]{:S(2)}) copy-start(f32[128,96]{1,0:T(8,128)} %get-tuple-element.145) | copy-start | bytes 147460
  790.2 19.1 %copy-start.5 = (f32[128,1024]{1,0:T(8,128)S(1)}, f32[128,1024]{1,0:T(8,128)}, u32[]{:S(2)}) copy-start(f32[128,1024]{1,0:T(8,128)} %copy-done.4) | copy-start | bytes 1572868
  790.2 19.1 %copy-start.46 = (f32[128,96]{1,0:T(8,128)S(1)}, f32[128,96]{1,0:T(8,128)}, u32[]{:S(2)}) copy-start(f32[128,96]{1,0:T(8,128)} %copy-done.45) | copy-start | bytes 147460
  980.5 70.6 %all-reduce.6.cloned.1.call-start = ((), (), s32[]{:S(2)}) async-start(), calls=%async_computation.7 | async-start | bytes 196608 | tf_op jit(solution)/shard_map/psum | solution.py:111
  1154.6 17.6 %copy-start.53 = (f32[128,96]{1,0:T(8,128)S(1)}, f32[128,96]{1,0:T(8,128)}, u32[]{:S(2)}) copy-start(f32[128,96]{1,0:T(8,128)} %copy-done.51) | copy-start | bytes 147460
  1172.3 17.6 %copy-start.50 = (f32[128,96]{1,0:T(8,128)S(1)}, f32[128,96]{1,0:T(8,128)}, u32[]{:S(2)}) copy-start(f32[128,96]{1,0:T(8,128)} %copy-done.48) | copy-start | bytes 147460
  1189.9 18.9 %copy-start.47 = (f32[128,96]{1,0:T(8,128)S(1)}, f32[128,96]{1,0:T(8,128)}, u32[]{:S(2)}) copy-start(f32[128,96]{1,0:T(8,128)} %copy-done.45) | copy-start | bytes 147460
  (70 other events, 659.0 us)
Sparse Core Ops, SparseCore 0:
  200.6 36.4 reduce-scatter.14
  386.7 36.4 reduce-scatter.12
  560.4 37.6 reduce-scatter.8
  600.3 34.4 all-reduce.3
  980.6 33.7 reduce-scatter.10
  1016.6 34.4 all-reduce.5
where the time goes:
time: 1240 us; the launch traced here: 1230 us
  matrix products  445 us (36%)
  other arithmetic  408 us (33%)
  local copies, waits for them, and re-layouts  211 us (17%)
  waiting for transfers between devices  112 us (9%)
  blocking collectives  41.1 us (3%)
  between operations  16.3 us (1%)
    reduce_sum x16, other arithmetic, forward(): col_sum = col_sum + jnp.sum(footprint, axis=1, dtype=jnp.float32)  296 us
    dot_general x16, matrix products, backward(): jnp.einsum('brv,brs->bsv', footprint, picked, preferred_element_type=jnp....  233 us
    dot_general x16, matrix products, forward(): jnp.einsum('brv,bsv->brs', footprint, rounded, preferred_element_type=jnp...  212 us
    reshape x16, local copies, waits for them, and re-layouts, forward(): contrib.reshape(2 * blocks, RAYS_TILE * slices)  86.8 us
    psum x2, waiting for transfers between devices, shards(): proj_total, raysum_total = lax.psum((proj_slab, raysum_slab), 'group')  73 us
    reshape x16, local copies, waits for them, and re-layouts, backward(): residual_b[tile_rows(angle, first_tile)]  67.6 us
    scatter-add x16, other arithmetic, forward(): projection.at[row_ids].add(contrib.reshape(2 * blocks, RAYS_TILE * slices))  40.7 us
    reduce_scatter x2, waiting for transfers between devices, shards(): lax.psum_scatter(projection, 'patch', scatter_dimension=0, tiled=True)  39.4 us
  transfers between devices with their start and end apart: 6, of which 4 were waited for; matrix products, arithmetic and copies ran while one was open for 30% of the time, Pallas kernels for 0%

commit v1 on v0

v1 whole, which is shorter than its diff:
```python
import math

import jax
import jax.numpy as jnp
import numpy as np
from jax import lax
from jax.experimental import pallas as pl
from jax.experimental.pallas import tpu as pltpu
from jax.sharding import PartitionSpec as P

IMG_BLK = 64
BLK_SIDE = 32
RAYS_TILE = 48
NTILE = 64
ANG_SUB = 8
SUBSETS = 2

spread = 1.5
relax = 0.9

SUB = 8
NQ = (BLK_SIDE // SUB) ** 2
R = 16
VOX = BLK_SIDE * BLK_SIDE
RAYS = NTILE * RAYS_TILE
LANES = 128
PAD = 32
TALL = RAYS + 2 * PAD
SPAN = 128
VMEM_LIMIT = 60 * 1024 * 1024


def angles(subset):
    return [math.pi * (a * SUBSETS + subset) / (ANG_SUB * SUBSETS) for a in range(ANG_SUB)]


def geometry(subset):
    v = np.arange(VOX)
    col = (v % BLK_SIDE) + 0.5 - BLK_SIDE / 2
    row = (v // BLK_SIDE) + 0.5 - BLK_SIDE / 2
    q_of = (v // BLK_SIDE // SUB) * (BLK_SIDE // SUB) + (v % BLK_SIDE) // SUB
    base = np.zeros((ANG_SUB, VOX), np.float64)
    first = np.zeros((ANG_SUB, NQ), np.int64)
    for a, theta in enumerate(angles(subset)):
        off = col * math.cos(theta) + row * math.sin(theta)
        for q in range(NQ):
            mine = q_of == q
            first[a, q] = math.floor(off[mine].min() - spread)
            base[a, mine] = off[mine] - first[a, q]
    return base.astype(np.float32), first.astype(np.int32)


def fill_grid(base_ref, e_scr):
    ray = lax.broadcasted_iota(jnp.int32, (R, VOX), 0).astype(jnp.float32)
    for a in range(ANG_SUB):
        e_scr[a * R:(a + 1) * R, :] = (base_ref[a:a + 1, :] - ray) * (1.0 / spread)


def make_footprint(e_scr, f_scr, frac_ref, b):
    for a in range(ANG_SUB):
        t = e_scr[a * R:(a + 1) * R, :] + frac_ref[b, a]
        bump = jnp.maximum(1.0 - t * t, 0.0)
        f_scr[a * R:(a + 1) * R, :] = (bump * bump).astype(jnp.bfloat16)


def merge_range(win_ref, a):
    begin = jnp.maximum(win_ref[0, a] - PAD, 0) // SPAN
    end = jnp.minimum((win_ref[1, a] + R + PAD) // SPAN + 1, RAYS // SPAN)
    return begin, end


def aligned(x, m):
    return pl.multiple_of(x, m)


def forward_kernel(nb, lo_ref, frac_ref, win_ref, first_ref, vol_ref, base_ref, out_ref,
                   e_scr, f_scr, m_scr, acc):
    step = pl.program_id(0)

    @pl.when(step == 0)
    def _():
        fill_grid(base_ref, e_scr)
        v = lax.broadcasted_iota(jnp.int32, (LANES, VOX), 1)
        line = lax.broadcasted_iota(jnp.int32, (LANES, VOX), 0)
        q_of = (v // (BLK_SIDE * SUB)) * (BLK_SIDE // SUB) + (v % BLK_SIDE) // SUB
        m_scr[...] = jnp.where(q_of == line // 8, 1.0, 0.0).astype(jnp.bfloat16)
        zero = jnp.zeros((64, LANES), jnp.float32)

        def clear_angle(a, c):
            begin, end = merge_range(win_ref, a)
            begin = begin * (SPAN // 64)
            end = end * (SPAN // 64) + 1

            def clear(i, c):
                acc[pl.ds(aligned(a * TALL + i * 64, 64), 64), :] = zero
                return c

            return lax.fori_loop(begin, end, clear, c)

        lax.fori_loop(0, ANG_SUB, clear_angle, 0)

    def one(i, c):
        b = step * nb + i
        make_footprint(e_scr, f_scr, frac_ref, b)
        rounded = vol_ref[i].astype(jnp.bfloat16)
        spreadv = jnp.tile(rounded, (NQ, 1)) * m_scr[...]
        part = lax.dot_general(f_scr[...], spreadv, (((1,), (1,)), ((), ())),
                               preferred_element_type=jnp.float32)
        for a in range(ANG_SUB):
            at = pl.ds(a * TALL + PAD + lo_ref[b, a], R)
            acc[at, :] += part[a * R:(a + 1) * R, :]
        return c

    lax.fori_loop(0, nb, one, 0, unroll=2)

    @pl.when(step == pl.num_programs(0) - 1)
    def _():
        out_ref[...] = jnp.zeros_like(out_ref)
        span = SPAN
        lane_q = lax.broadcasted_iota(jnp.int32, (span, LANES), 1) // 8
        row_j = lax.broadcasted_iota(jnp.int32, (span, LANES), 0) % 16
        pick = lane_q == row_j

        def merge_angle(a, c):
            begin, end = merge_range(win_ref, a)

            def merge(i, c):
                k = i * span
                total = jnp.zeros((span, LANES), jnp.float32)
                for q in range(NQ):
                    src = a * TALL + PAD + k - first_ref[a, q]
                    total = jnp.where(lane_q == q, acc[pl.ds(src, span), :], total)
                for s in (64, 32, 16, 8):
                    total = total + pltpu.roll(total, s, 1)
                total = jnp.where(pick, total, 0.0)
                out = jnp.sum(total.reshape(span // 16, 16, LANES), axis=1)
                out_ref[pl.ds(aligned(a * (RAYS // 16) + i * 8, 8), 8), :] = out
                return c

            return lax.fori_loop(begin, end, merge, c)

        lax.fori_loop(0, ANG_SUB, merge_angle, 0)


def backward_kernel(nb, lo_ref, frac_ref, win_ref, first_ref, vol_ref, base_ref, res_ref, out_ref,
                    e_scr, f_scr, rb, dd):
    step = pl.program_id(0)

    @pl.when(step == 0)
    def _():
        fill_grid(base_ref, e_scr)
        span = SPAN
        lane_q = lax.broadcasted_iota(jnp.int32, (span, LANES), 1) // 8
        row_j = lax.broadcasted_iota(jnp.int32, (span, LANES), 0) % 16
        pick = lane_q == row_j
        fold = jnp.where(
            lax.broadcasted_iota(jnp.int32, (LANES, LANES), 0) % 8
            == lax.broadcasted_iota(jnp.int32, (LANES, LANES), 1) % 8, 1.0, 0.0).astype(jnp.bfloat16)

        def one_angle(a, c):
            begin = jnp.maximum((win_ref[0, a] - 64) // span, 0)
            end = jnp.minimum((win_ref[1, a] + 64 + span) // span + 1, RAYS // span)

            def widen(i, c):
                rows = res_ref[pl.ds(aligned(a * (RAYS // 16) + i * 8, 8), 8), :]
                wide = jnp.broadcast_to(rows[:, None, :], (8, 16, LANES)).reshape(span, LANES)
                wide = jnp.where(pick, wide, 0.0).astype(jnp.bfloat16)
                rb[pl.ds(aligned(PAD + i * span, 8), span), :] = jnp.dot(
                    wide, fold, preferred_element_type=jnp.float32)
                return c

            lax.fori_loop(begin, end, widen, 0)
            first = jnp.maximum(win_ref[0, a] // span, 0)
            last = jnp.minimum((win_ref[1, a] + 16) // span + 1, RAYS // span)

            def shift(i, c):
                k = i * span
                total = jnp.zeros((span, LANES), jnp.float32)
                for q in range(NQ):
                    src = PAD + k + first_ref[a, q]
                    total = jnp.where(lane_q == q, rb[pl.ds(src, span), :], total)
                dd[pl.ds(aligned(a * RAYS + k, span), span), :] = total
                return c

            lax.fori_loop(first, last, shift, 0)
            return c

        lax.fori_loop(0, ANG_SUB, one_angle, 0)

    width = SUB * BLK_SIDE
    group = BLK_SIDE // SUB
    lane = lax.broadcasted_iota(jnp.int32, (8, width), 1)
    col_group = (lane % BLK_SIDE) // SUB

    def one(i, c):
        b = step * nb + i
        make_footprint(e_scr, f_scr, frac_ref, b)
        rows = jnp.concatenate(
            [dd[pl.ds(a * RAYS + lo_ref[b, a], R), :] for a in range(ANG_SUB)], axis=0)
        turned = jnp.transpose(rows)
        ones = jnp.ones((8, ANG_SUB * R), jnp.float32)
        for g in range(group):
            lhs = jnp.concatenate([turned[g * 32:(g + 1) * 32], ones], axis=0).astype(jnp.bfloat16)
            at = slice(g * width, (g + 1) * width)
            part = jnp.dot(lhs, f_scr[:, at], preferred_element_type=jnp.float32)
            back = part[0:8]
            for j in range(1, group):
                back = jnp.where(col_group == j, part[j * 8:(j + 1) * 8], back)
            col_sum = part[32:40]
            out_ref[i, :, at] = jnp.maximum(vol_ref[i, :, at] + relax * back / col_sum, 0.0)
        return c

    lax.fori_loop(0, nb, one, 0, unroll=2)


def ray_sum_kernel(c_ref, s_ref, k_ref, out_ref):
    side = IMG_BLK * BLK_SIDE
    half = side * 0.5
    for u in range(c_ref.shape[0]):
        cs = c_ref[u] * (1.0 / spread)
        sn = s_ref[u] * (1.0 / spread)
        inv = 1.0 / cs
        ray = k_ref[u] * (1.0 / spread)

        def row(i, total):
            y = i.astype(jnp.float32) + (0.5 - half)
            w = ray - y * sn
            mid = jnp.floor(w * inv) + 0.5
            t0 = mid * cs - w
            for j in range(-2, 3):
                t = t0 + j * cs
                bump = jnp.maximum(1.0 - t * t, 0.0)
                total = total + jnp.where(jnp.abs(mid + j) < half, bump * bump, 0.0)
            return total

        out_ref[u] = lax.fori_loop(0, side, row, jnp.zeros(out_ref.shape[1:], jnp.float32), unroll=8)


def smem():
    return pl.BlockSpec(memory_space=pltpu.SMEM)


def forward(volume, lo, frac, win, base, first):
    blocks, slices, _ = volume.shape
    nb = 8
    lines = ANG_SUB * RAYS // 16
    return pl.pallas_call(
        lambda *refs: forward_kernel(nb, *refs),
        grid=(blocks // nb,),
        in_specs=[smem(), smem(), smem(), smem(),
                  pl.BlockSpec((nb, slices, VOX), lambda i: (i, 0, 0)),
                  pl.BlockSpec((ANG_SUB, VOX), lambda i: (0, 0))],
        out_specs=pl.BlockSpec((lines, LANES), lambda i: (0, 0)),
        out_shape=jax.ShapeDtypeStruct((lines, LANES), jnp.float32),
        scratch_shapes=[pltpu.VMEM((ANG_SUB * R, VOX), jnp.float32),
                        pltpu.VMEM((ANG_SUB * R, VOX), jnp.bfloat16),
                        pltpu.VMEM((LANES, VOX), jnp.bfloat16),
                        pltpu.VMEM((ANG_SUB * TALL, LANES), jnp.float32)],
        compiler_params=pltpu.CompilerParams(vmem_limit_bytes=VMEM_LIMIT),
        name="forward",
    )(lo, frac, win, first, volume, base)


def backward(volume, residual, lo, frac, win, base, first):
    blocks, slices, _ = volume.shape
    nb = 8
    return pl.pallas_call(
        lambda *refs: backward_kernel(nb, *refs),
        grid=(blocks // nb,),
        in_specs=[smem(), smem(), smem(), smem(),
                  pl.BlockSpec((nb, slices, VOX), lambda i: (i, 0, 0)),
                  pl.BlockSpec((ANG_SUB, VOX), lambda i: (0, 0)),
                  pl.BlockSpec(residual.shape, lambda i: (0, 0))],
        out_specs=pl.BlockSpec((nb, slices, VOX), lambda i: (i, 0, 0)),
        out_shape=jax.ShapeDtypeStruct(volume.shape, jnp.float32),
        scratch_shapes=[pltpu.VMEM((ANG_SUB * R, VOX), jnp.float32),
                        pltpu.VMEM((ANG_SUB * R, VOX), jnp.bfloat16),
                        pltpu.VMEM((TALL, LANES), jnp.float32),
                        pltpu.VMEM((ANG_SUB * RAYS, LANES), jnp.float32)],
        compiler_params=pltpu.CompilerParams(vmem_limit_bytes=VMEM_LIMIT),
        name="backward",
    )(lo, frac, win, first, volume, base, residual)


def own_ray_sums(first_row, rows):
    count = rows * RAYS_TILE
    padded = -(-count // 1024) * 1024
    idx = jnp.minimum(jnp.arange(padded, dtype=jnp.int32), count - 1)
    row = first_row + idx // RAYS_TILE
    ray = ((row % NTILE) * RAYS_TILE + idx % RAYS_TILE).astype(jnp.float32) + (0.5 - RAYS * 0.5)
    angle = row // NTILE
    big, small = [], []
    for subset in range(SUBSETS):
        th = angles(subset)
        pairs = [sorted((math.cos(t), math.sin(t)), key=abs) for t in th]
        sign = jnp.zeros((padded,), jnp.float32)
        b, s = sign, sign
        for a in range(ANG_SUB):
            b = jnp.where(angle == a, np.float32(pairs[a][1]), b)
            s = jnp.where(angle == a, np.float32(pairs[a][0]), s)
        big.append(b)
        small.append(s)
    shape = (SUBSETS, padded // LANES, LANES)
    big = jnp.stack(big).reshape(shape)
    small = jnp.stack(small).reshape(shape)
    rays = jnp.broadcast_to(ray.reshape(1, padded // LANES, LANES), shape)
    sums = pl.pallas_call(
        ray_sum_kernel,
        out_shape=jax.ShapeDtypeStruct(shape, jnp.float32),
        name="raysum",
    )(big, small, rays)
    return sums.reshape(SUBSETS, padded)[:, :count]


def placing(place, subset):
    half = IMG_BLK * BLK_SIDE * 0.5
    x = (place % IMG_BLK).astype(jnp.float32) * BLK_SIDE + (BLK_SIDE * 0.5 - half)
    y = (place // IMG_BLK).astype(jnp.float32) * BLK_SIDE + (BLK_SIDE * 0.5 - half)
    cosine = np.cos(np.array(angles(subset))).astype(np.float32)
    sine = np.sin(np.array(angles(subset))).astype(np.float32)
    z = x[:, None] * cosine + y[:, None] * sine + (RAYS * 0.5 - 0.5)
    low = jnp.floor(z)
    lo = low.astype(jnp.int32)
    win = jnp.stack([jnp.min(lo, axis=0), jnp.max(lo, axis=0)])
    return lo, (z - low) * (1.0 / spread), win


def shards(volume, block_place, measured, live_rays):
    groups = lax.axis_size("group")
    patches = lax.axis_size("patch")
    group_index = lax.axis_index("group")
    patch_index = lax.axis_index("patch")
    slices = volume.shape[1]
    slab_rows = ANG_SUB * NTILE // patches
    rows = slab_rows // groups
    first_row = patch_index * slab_rows + group_index * rows
    lines = rows * RAYS_TILE * slices // LANES
    per = LANES // slices
    sums = own_ray_sums(first_row, rows)
    estimate = volume
    own_residual = None
    for subset in range(SUBSETS):
        base, first = geometry(subset)
        lo, frac, win = placing(block_place, subset)
        partial = forward(estimate, lo, frac, win, base, first)
        total = lax.psum_scatter(partial, ("patch", "group"), scatter_dimension=0, tiled=True)
        mine = lax.dynamic_slice_in_dim(measured[subset], group_index * rows, rows, 0)
        live = lax.dynamic_slice_in_dim(live_rays[subset], first_row, rows, 0)
        on = jnp.arange(RAYS_TILE, dtype=jnp.int32)[None, :] < live[:, None]
        on = jnp.broadcast_to(on[:, :, None], (rows, RAYS_TILE, slices)).reshape(lines, LANES)
        rs = jnp.maximum(sums[subset], 1.0).reshape(lines, per, 1)
        rs = jnp.broadcast_to(rs, (lines, per, slices)).reshape(lines, LANES)
        residual = jnp.where(on, mine.reshape(lines, LANES) - total / rs, 0.0)
        own_residual = residual.reshape(rows, RAYS_TILE * slices)
        full = lax.all_gather(residual.astype(jnp.bfloat16), ("patch", "group"), axis=0, tiled=True)
        estimate = backward(estimate, full.astype(jnp.float32), lo, frac, win, base, first)
    return (estimate, own_residual[None])


def solution(mesh):
    return jax.shard_map(
        shards,
        mesh=mesh,
        in_specs=(
            P(("group", "patch"), None, None),
            P(("group", "patch")),
            P(None, "patch", None),
            P(),
        ),
        out_specs=(P(("group", "patch"), None, None), P("group", "patch", None)),
        check_vma=False,
    )
```

time: 1240 us -> 578 us (0.47)
  matrix products: 445 us -> 0 us
  other arithmetic: 408 us -> 9.05 us
  Pallas kernels: 0 us -> 279 us
  local copies, waits for them, and re-layouts: 211 us -> 3.3 us
  blocking collectives: 41.1 us -> 136 us
  waiting for transfers between devices: 112 us -> 143 us
    dot_general x32 -> x0, matrix products: 445 us -> none  [the longest x16 233 us: backward(): jnp.einsum('brv,brs->bsv', footprint, picked, preferred_element_type=jnp....]
    reduce_sum x16 -> x0, other arithmetic: 296 us -> none  [forward(): col_sum = col_sum + jnp.sum(footprint, axis=1, dtype=jnp.float32)]
    pallas_call x0 -> x5, Pallas kernels: none -> 279 us  [the longest x2 139 us: forward(): pl.pallas_call(lambda *refs: forward_kernel(nb, *refs), grid=(blocks // n...]
    reshape x48 -> x8, local copies, waits for them, and re-layouts: 166 us -> 0.6 us  [the longest x2 0.44 us: shards(): jnp.broadcast_to(on[:, :, None], (rows, RAYS_TILE, slices))]
    all_gather x2, blocking collectives: 19.1 us -> 136 us  [shards(): lax.all_gather(residual.astype(jnp.bfloat16), ('patch', 'group'), axis=0,...]
    reduce_scatter x2, waiting for transfers between devices: 39.4 us -> 143 us  [shards(): lax.psum_scatter(partial, ('patch', 'group'), scatter_dimension=0, tiled=...]
    scatter-add x32 -> x0, other arithmetic: 75.2 us -> none  [the longest x16 40.7 us: forward(): projection.at[row_ids].add(contrib.reshape(2 * blocks, RAYS_TILE * slices))]
    psum x2 -> x0, waiting for transfers between devices: 73 us -> none  [shards(): proj_total, raysum_total = lax.psum((proj_slab, raysum_slab), 'group')]
  transfers between devices with their start and end apart: 6 -> 2, of which waited for: 4 -> 2; matrix products, arithmetic and copies ran while one was open for 30% -> 1% of each run, Pallas kernels for 0% -> 6%
where the time goes in v1:
time: 578 us; the launch traced here: 585 us
  Pallas kernels  279 us (48%)
  waiting for transfers between devices  143 us (25%)
  blocking collectives  136 us (24%)
  between operations  14.2 us (2%)
  other arithmetic  9.05 us (2%)
    reduce_scatter x2, waiting for transfers between devices, shards(): lax.psum_scatter(partial, ('patch', 'group'), scatter_dimension=0, tiled=...  143 us
    pallas_call x2, Pallas kernels, forward(): pl.pallas_call(lambda *refs: forward_kernel(nb, *refs), grid=(blocks // n...  139 us
    all_gather x2, blocking collectives, shards(): lax.all_gather(residual.astype(jnp.bfloat16), ('patch', 'group'), axis=0,...  136 us
    pallas_call x2, Pallas kernels, backward(): pl.pallas_call(lambda *refs: backward_kernel(nb, *refs), grid=(blocks //...  103 us
    pallas_call x1, Pallas kernels, own_ray_sums(): pl.pallas_call(ray_sum_kernel, out_shape=jax.ShapeDtypeStruct(shape, jnp....  36.6 us
  transfers between devices with their start and end apart: 2, of which 2 were waited for; matrix products, arithmetic and copies ran while one was open for 1% of the time, Pallas kernels for 6%

profile of v1, /device:TPU:0, one launch (start us, length us, event | category | flops | bytes accessed | tf_op | source)
XLA Modules:
  0.0 584.5 jit_solution(5141438060719353282)
XLA Ops:
  7.2 0.0 copy-start.1
  7.2 0.0 copy-start
  7.2 0.0 reduce-scatter.3.cloned.1.call-start
  7.2 0.7 multiply_add_fusion
  7.9 0.8 fusion.5
  8.8 1.5 fusion.1
  10.3 0.6 pad_add_fusion.1.refs_2_
  10.9 69.4 %forward.2 = f32[1536,128]{1,0:T(8,128)} custom-call(s32[128,8]{1,0:T(8,128)} %get-tuple-element.17.refs_0_, f32[128,8]{1,0:T(8,128)} %get-tuple-element.16.refs_1_, s32[2,8]{1,0:T(2,128)} %pad_add_fusion.1.refs_2_, s32[8,16]{1,0:T(8,128)} %constant.169.clone.refs_3_, f32[128,8,1024]{2,1,0:T(8,128)} %refs_4_.3, f32[8,1024]{1,0:T(8,128)} %constant.170.clone.refs_5_), custom_call_target="tpu_custom_call" | custom-call | tf_op jit(solution)/shard_map/forward/pallas_call | solution.py:247
  80.3 0.0 reduce-scatter.3.cloned.1.call-update
  80.3 0.0 reduce-scatter.5.cloned.1.call-start
  80.5 0.6 pad_maximum_fusion.1.s_ref
  81.0 0.6 pad_maximum_fusion.c_ref
  81.6 0.6 broadcast_in_dim.126.k_ref
  82.2 36.6 %raysum.1 = f32[2,8,128]{2,1,0:T(8,128)} custom-call(f32[2,8,128]{2,1,0:T(8,128)} %pad_maximum_fusion.c_ref, f32[2,8,128]{2,1,0:T(8,128)} %pad_maximum_fusion.1.s_ref, f32[2,8,128]{2,1,0:T(8,128)} %broadcast_in_dim.126.k_ref), custom_call_target="tpu_custom_call" | custom-call | tf_op jit(solution)/shard_map/raysum/pallas_call | solution.py:307
  118.9 0.7 copy.26
  119.6 0.1 max.21
  119.7 0.1 copy.20
  119.7 0.1 copy.21
  119.8 0.0 copy-done.1
  119.8 0.1 fusion.23
  119.9 0.1 iota_compare_fusion.1
  120.0 0.2 broadcast_in_dim.109
  120.2 0.2 reshape.344
  120.4 0.0 copy-done
  120.5 0.5 pad_add_fusion.refs_2_
  121.0 51.5 %reduce-scatter.3.cloned.1.call-done = f32[48,128]{1,0:T(8,128)} async-done(((f32[1536,128]{1,0:T(8,128)}), f32[48,128]{1,0:T(8,128)}) %reduce-scatter.3.cloned.1.call-update) | async-done | bytes 24592 | tf_op jit(solution)/shard_map/reduce_scatter | solution.py:346
  172.5 0.7 select_convert_fusion
  173.3 68.1 %all_gather.6 = bf16[1536,128]{1,0:T(8,128)(2,1)S(1)} all-gather(bf16[48,128]{1,0:T(8,128)(2,1)S(1)} %select_convert_fusion), channel_id=1, replica_groups=mesh['group'=4,'patch'=8] {'patch','group'}, dimensions={0}, use_global_device_ids=true | all-gather | bytes 405504 | tf_op jit(solution)/shard_map/all_gather | solution.py:355
  241.4 0.9 convert_element_type.39.refs_6_
  242.3 51.5 %backward.2.refs_4_ = f32[128,8,1024]{2,1,0:T(8,128)} custom-call(s32[128,8]{1,0:T(8,128)} %get-tuple-element.17.refs_0_, f32[128,8]{1,0:T(8,128)} %get-tuple-element.16.refs_1_, s32[2,8]{1,0:T(2,128)} %pad_add_fusion.1.refs_2_, s32[8,16]{1,0:T(8,128)} %constant.169.clone.refs_3_, f32[128,8,1024]{2,1,0:T(8,128)} %refs_4_.3, ...), custom_call_target="tpu_custom_call" | custom-call | tf_op jit(solution)/shard_map/backward/pallas_call | solution.py:267
  293.9 69.6 %forward.3 = f32[1536,128]{1,0:T(8,128)} custom-call(s32[128,8]{1,0:T(8,128)} %get-tuple-element.20.refs_0_, f32[128,8]{1,0:T(8,128)} %get-tuple-element.21.refs_1_, s32[2,8]{1,0:T(2,128)} %pad_add_fusion.refs_2_, s32[8,16]{1,0:T(8,128)} %constant.173.clone.refs_3_, f32[128,8,1024]{2,1,0:T(8,128)} %backward.2.refs_4_, f32[8,1024]{1,0:T(8,128)} %constant.174.clone.refs_5_), custom_call_target="tpu_custom_call" | custom-call | tf_op jit(solution)/shard_map/forward/pallas_call | solution.py:247
  363.5 0.0 reduce-scatter.5.cloned.1.call-update
  363.5 0.1 max.23
  363.6 0.1 copy.22
  363.7 0.1 copy.23
  363.8 0.1 iota_compare_fusion
  363.8 0.2 broadcast_in_dim.129
  364.0 0.2 reshape.348
  364.3 91.5 %reduce-scatter.5.cloned.1.call-done = f32[48,128]{1,0:T(8,128)} async-done(((f32[1536,128]{1,0:T(8,128)}), f32[48,128]{1,0:T(8,128)}) %reduce-scatter.5.cloned.1.call-update) | async-done | bytes 24592 | tf_op jit(solution)/shard_map/reduce_scatter | solution.py:346
  455.8 0.8 fusion.28
  456.6 0.6 broadcast_in_dim_reshape.3
  457.2 68.1 %all_gather.7 = bf16[1536,128]{1,0:T(8,128)(2,1)S(1)} all-gather(bf16[48,128]{1,0:T(8,128)(2,1)S(1)} %get-tuple-element.10), channel_id=1, replica_groups=mesh['group'=4,'patch'=8] {'patch','group'}, dimensions={0}, use_global_device_ids=true | all-gather | bytes 405504 | tf_op jit(solution)/shard_map/all_gather | solution.py:355
  525.3 0.9 convert_element_type.41.refs_6_
  526.2 51.5 %backward.3 = f32[128,8,1024]{2,1,0:T(8,128)} custom-call(s32[128,8]{1,0:T(8,128)} %get-tuple-element.20.refs_0_, f32[128,8]{1,0:T(8,128)} %get-tuple-element.21.refs_1_, s32[2,8]{1,0:T(2,128)} %pad_add_fusion.refs_2_, s32[8,16]{1,0:T(8,128)} %constant.173.clone.refs_3_, f32[128,8,1024]{2,1,0:T(8,128)} %backward.2.refs_4_, ...), custom_call_target="tpu_custom_call" | custom-call | tf_op jit(solution)/shard_map/backward/pallas_call | solution.py:267
  (12 shorter events, 0.2 us)
Async XLA Ops:
  7.2 112.6 %copy-start.1 = (s32[2,512]{1,0:T(2,128)S(1)}, s32[2,512]{1,0:T(2,128)}, u32[]{:S(2)}) copy-start(s32[2,512]{1,0:T(2,128)} %param.15) | copy-start | bytes 12292
  7.2 113.2 %copy-start = (f32[2,64,384]{2,1,0:T(8,128)S(1)}, f32[2,64,384]{2,1,0:T(8,128)}, u32[]{:S(2)}) copy-start(f32[2,64,384]{2,1,0:T(8,128)} %param.14) | copy-start | bytes 589828
  7.2 165.4 %reduce-scatter.3.cloned.1.call-start = ((), (), s32[]{:S(2)}) async-start(), calls=%async_computation.2 | async-start | bytes 811008 | tf_op jit(solution)/shard_map/reduce_scatter | solution.py:346
  80.3 375.5 %reduce-scatter.5.cloned.1.call-start = ((), (), s32[]{:S(2)}) async-start(), calls=%async_computation.3 | async-start | bytes 811008 | tf_op jit(solution)/shard_map/reduce_scatter | solution.py:346
Sparse Core Ops, SparseCore 0:
  80.4 92.0 reduce-scatter.2
  363.7 92.1 reduce-scatter.4

commit v2 on v1

--- a/solution.py
+++ b/solution.py
@@ -234,6 +234,116 @@
             return total
 
         out_ref[u] = lax.fori_loop(0, side, row, jnp.zeros(out_ref.shape[1:], jnp.float32), unroll=8)
+
+
+def exchange_kernel(part_ref, mine_ref, on_ref, rs_ref, full_ref, own_ref,
+                    half, inbox, sums, stage, gathered, send_sem, recv_sem,
+                    pair_send, pair_recv, out_send, out_recv, back_send, back_recv):
+    g, p = lax.axis_index("group"), lax.axis_index("patch")
+    groups, pairs = inbox.shape[1], inbox.shape[0]
+    n = groups * pairs
+    parity, column = lax.rem(p, 2), p // 2
+    me = column * groups + g
+    partner = (g, column * 2 + 1 - parity)
+    mesh_id = pl.DeviceIdType.MESH
+
+    def peer(d):
+        at = lax.rem(me + d, n)
+        return at // groups, lax.rem(at, groups)
+
+    barrier = pltpu.get_barrier_semaphore()
+    pl.semaphore_signal(barrier, inc=1, device_id=partner, device_id_type=mesh_id)
+
+    def greet(d, c):
+        pc, pg = peer(d)
+        pl.semaphore_signal(barrier, inc=1, device_id=(pg, pc * 2 + parity), device_id_type=mesh_id)
+        return c
+
+    lax.fori_loop(1, n, greet, 0)
+    pl.semaphore_wait(barrier, n)
+
+    swap = pltpu.make_async_remote_copy(
+        src_ref=part_ref.at[:, 1 - parity], dst_ref=half, send_sem=pair_send, recv_sem=pair_recv,
+        device_id=partner, device_id_type=mesh_id)
+    swap.start()
+    swap.wait()
+    for i in range(pairs):
+        sums[i] = part_ref[i, parity] + half[i]
+
+    def to_owner(d):
+        pc, pg = peer(d)
+        return pltpu.make_async_remote_copy(
+            src_ref=sums.at[pc, pg], dst_ref=inbox.at[column, g], send_sem=send_sem.at[d],
+            recv_sem=recv_sem.at[d], device_id=(pg, pc * 2 + parity), device_id_type=mesh_id)
+
+    def go(d, c):
+        to_owner(d).start()
+        return c
+
+    def done(d, c):
+        to_owner(d).wait()
+        return c
+
+    lax.fori_loop(1, n, go, 0)
+    inbox[column, g] = sums[column, g]
+    lax.fori_loop(1, n, done, 0)
+    total = jnp.zeros(mine_ref.shape, jnp.float32)
+    for i in range(pairs):
+        for j in range(groups):
+            total = total + inbox[i, j]
+    residual = (mine_ref[...] - total / rs_ref[...]) * on_ref[...]
+    own_ref[...] = residual
+    stage[...] = residual.astype(jnp.bfloat16)
+
+    def to_all(d):
+        pc, pg = peer(d)
+        return pltpu.make_async_remote_copy(
+            src_ref=stage, dst_ref=gathered.at[column, parity, g], send_sem=out_send.at[d],
+            recv_sem=out_recv.at[d], device_id=(pg, pc * 2 + parity), device_id_type=mesh_id)
+
+    def go_all(d, c):
+        to_all(d).start()
+        return c
+
+    def done_all(d, c):
+        to_all(d).wait()
+        return c
+
+    lax.fori_loop(1, n, go_all, 0)
+    gathered[column, parity, g] = stage[...]
+    lax.fori_loop(1, n, done_all, 0)
+    share = pltpu.make_async_remote_copy(
+        src_ref=gathered.at[:, parity], dst_ref=gathered.at[:, parity], send_sem=back_send,
+        recv_sem=back_recv, device_id=partner, device_id_type=mesh_id)
+    share.start()
+    share.wait()
+    for i in range(pairs):
+        full_ref[i] = gathered[i].astype(jnp.float32)
+
+
+def exchange(partial, mine, on, rs, groups, patches):
+    lines = mine.shape[0]
+    pairs = patches // 2
+    shape = (pairs, 2, groups, lines, LANES)
+    n = pairs * groups
+    dma = pltpu.SemaphoreType.DMA
+    vmem = pl.BlockSpec(memory_space=pltpu.VMEM)
+    full, own = pl.pallas_call(
+        exchange_kernel,
+        in_specs=[vmem] * 4,
+        out_specs=[vmem] * 2,
+        out_shape=[jax.ShapeDtypeStruct(shape, jnp.float32),
+                   jax.ShapeDtypeStruct((lines, LANES), jnp.float32)],
+        scratch_shapes=[pltpu.VMEM((pairs, groups, lines, LANES), jnp.float32),
+                        pltpu.VMEM((pairs, groups, lines, LANES), jnp.float32),
+                        pltpu.VMEM((pairs, groups, lines, LANES), jnp.float32),
+                        pltpu.VMEM((lines, LANES), jnp.bfloat16),
+                        pltpu.VMEM(shape, jnp.bfloat16),
+                        dma((n,)), dma((n,)), dma, dma, dma((n,)), dma((n,)), dma, dma],
+        compiler_params=pltpu.CompilerParams(collective_id=0, has_side_effects=True),
+        name="exchange",
+    )(partial.reshape(shape), mine, on, rs)
+    return full.reshape(partial.shape), own
 
 
 def smem():
@@ -343,17 +453,15 @@
         base, first = geometry(subset)
         lo, frac, win = placing(block_place, subset)
         partial = forward(estimate, lo, frac, win, base, first)
-        total = lax.psum_scatter(partial, ("patch", "group"), scatter_dimension=0, tiled=True)
         mine = lax.dynamic_slice_in_dim(measured[subset], group_index * rows, rows, 0)
         live = lax.dynamic_slice_in_dim(live_rays[subset], first_row, rows, 0)
         on = jnp.arange(RAYS_TILE, dtype=jnp.int32)[None, :] < live[:, None]
         on = jnp.broadcast_to(on[:, :, None], (rows, RAYS_TILE, slices)).reshape(lines, LANES)
         rs = jnp.maximum(sums[subset], 1.0).reshape(lines, per, 1)
         rs = jnp.broadcast_to(rs, (lines, per, slices)).reshape(lines, LANES)
-        residual = jnp.where(on, mine.reshape(lines, LANES) - total / rs, 0.0)
-        own_residual = residual.reshape(rows, RAYS_TILE * slices)
-        full = lax.all_gather(residual.astype(jnp.bfloat16), ("patch", "group"), axis=0, tiled=True)
-        estimate = backward(estimate, full.astype(jnp.float32), lo, frac, win, base, first)
+        full, own = exchange(partial, mine.reshape(lines, LANES), on.astype(jnp.float32), rs, groups, patches)
+        own_residual = own.reshape(rows, RAYS_TILE * slices)
+        estimate = backward(estimate, full, lo, frac, win, base, first)
     return (estimate, own_residual[None])
 
 

time: 578 us -> 339 us (0.59)
  the two profiles are of different devices: /device:TPU:0 before, /device:TPU:9 now
where the time goes in v2:
time: 339 us; the launch traced here: 337 us
  Pallas kernels  322 us (95%)
  local copies, waits for them, and re-layouts  8.51 us (3%)
  other arithmetic  5.71 us (2%)
    pallas_call x2, Pallas kernels, forward(): pl.pallas_call(lambda *refs: forward_kernel(nb, *refs), grid=(blocks // n...  138 us
    pallas_call x2, Pallas kernels, backward(): pl.pallas_call(lambda *refs: backward_kernel(nb, *refs), grid=(blocks //...  103 us
    pallas_call x2, Pallas kernels, exchange(): pl.pallas_call(exchange_kernel, in_specs=[vmem] * 4, out_specs=[vmem] * 2...  45.3 us
    pallas_call x1, Pallas kernels, own_ray_sums(): pl.pallas_call(ray_sum_kernel, out_shape=jax.ShapeDtypeStruct(shape, jnp....  36.6 us

profile of v2, /device:TPU:9, one launch (start us, length us, event | category | flops | bytes accessed | tf_op | source)
XLA Modules:
  0.0 337.3 jit_solution(10917785861221800739)
XLA Ops:
  0.6 0.7 multiply_add_fusion
  1.3 0.8 fusion.5
  2.2 0.6 pad_add_fusion.1.refs_2_
  2.8 0.6 pad_add_fusion.refs_2_
  3.4 0.6 broadcast_in_dim.121.k_ref
  4.0 0.8 fusion.31
  4.7 0.1 fusion.25
  4.8 0.1 fusion.6
  4.9 0.1 fusion.7
  5.0 0.6 pad_maximum_fusion.1.s_ref
  5.6 0.6 pad_maximum_fusion.c_ref
  6.2 36.6 %raysum.1 = f32[2,8,128]{2,1,0:T(8,128)} custom-call(f32[2,8,128]{2,1,0:T(8,128)} %pad_maximum_fusion.c_ref, f32[2,8,128]{2,1,0:T(8,128)} %pad_maximum_fusion.1.s_ref, f32[2,8,128]{2,1,0:T(8,128)} %broadcast_in_dim.121.k_ref), custom_call_target="tpu_custom_call" | custom-call | tf_op jit(solution)/shard_map/raysum/pallas_call | solution.py:417
  42.9 0.7 copy.26
  43.6 0.1 max.23
  43.7 0.1 copy.22
  43.7 0.1 max.21
  43.8 0.1 copy.20
  43.9 0.7 copy.21.rs_ref
  44.6 0.7 copy.23.rs_ref
  45.3 1.0 fusion.30
  46.2 0.6 reshape.360.mine_ref
  46.8 0.6 reshape.355.mine_ref
  47.4 1.5 fusion.1
  49.0 0.2 broadcast_in_dim.123
  49.2 0.8 convert_element_type.39.on_ref
  49.9 0.2 broadcast_in_dim.104
  50.1 0.8 convert_element_type.36.on_ref
  50.9 68.5 %forward.2 = f32[1536,128]{1,0:T(8,128)} custom-call(s32[128,8]{1,0:T(8,128)} %get-tuple-element.21.refs_0_, f32[128,8]{1,0:T(8,128)} %get-tuple-element.20.refs_1_, s32[2,8]{1,0:T(2,128)} %pad_add_fusion.1.refs_2_, s32[8,16]{1,0:T(8,128)} %constant.169.clone.refs_3_, f32[128,8,1024]{2,1,0:T(8,128)} %refs_4_.3, f32[8,1024]{1,0:T(8,128)} %constant.170.clone.refs_5_), custom_call_target="tpu_custom_call" | custom-call | tf_op jit(solution)/shard_map/forward/pallas_call | solution.py:357
  119.4 22.6 %exchange.2 = (f32[4,2,4,48,128]{4,3,2,1,0:T(8,128)}, f32[48,128]{1,0:T(8,128)}) custom-call(f32[4,2,4,48,128]{4,3,2,1,0:T(8,128)} %bitcast.20, f32[48,128]{1,0:T(8,128)} %reshape.355.mine_ref, f32[48,128]{1,0:T(8,128)} %convert_element_type.36.on_ref, f32[48,128]{1,0:T(8,128)} %copy.21.rs_ref), custom_call_target="tpu_custom_call" | custom-call | tf_op jit(solution)/shard_map/exchange/pallas_call | solution.py:331
  142.1 51.4 %backward.2.refs_4_ = f32[128,8,1024]{2,1,0:T(8,128)} custom-call(s32[128,8]{1,0:T(8,128)} %get-tuple-element.21.refs_0_, f32[128,8]{1,0:T(8,128)} %get-tuple-element.20.refs_1_, s32[2,8]{1,0:T(2,128)} %pad_add_fusion.1.refs_2_, s32[8,16]{1,0:T(8,128)} %constant.169.clone.refs_3_, f32[128,8,1024]{2,1,0:T(8,128)} %refs_4_.3, ...), custom_call_target="tpu_custom_call" | custom-call | tf_op jit(solution)/shard_map/backward/pallas_call | solution.py:377
  193.5 69.2 %forward.3 = f32[1536,128]{1,0:T(8,128)} custom-call(s32[128,8]{1,0:T(8,128)} %get-tuple-element.24.refs_0_, f32[128,8]{1,0:T(8,128)} %get-tuple-element.25.refs_1_, s32[2,8]{1,0:T(2,128)} %pad_add_fusion.refs_2_, s32[8,16]{1,0:T(8,128)} %constant.173.clone.refs_3_, f32[128,8,1024]{2,1,0:T(8,128)} %backward.2.refs_4_, f32[8,1024]{1,0:T(8,128)} %constant.174.clone.refs_5_), custom_call_target="tpu_custom_call" | custom-call | tf_op jit(solution)/shard_map/forward/pallas_call | solution.py:357
  262.7 22.6 %exchange.3 = (f32[4,2,4,48,128]{4,3,2,1,0:T(8,128)}, f32[48,128]{1,0:T(8,128)}) custom-call(f32[4,2,4,48,128]{4,3,2,1,0:T(8,128)} %bitcast.21, f32[48,128]{1,0:T(8,128)} %reshape.360.mine_ref, f32[48,128]{1,0:T(8,128)} %convert_element_type.39.on_ref, f32[48,128]{1,0:T(8,128)} %copy.23.rs_ref), custom_call_target="tpu_custom_call" | custom-call | tf_op jit(solution)/shard_map/exchange/pallas_call | solution.py:331
  285.4 0.0 copy-start
  285.4 51.3 %backward.3 = f32[128,8,1024]{2,1,0:T(8,128)} custom-call(s32[128,8]{1,0:T(8,128)} %get-tuple-element.24.refs_0_, f32[128,8]{1,0:T(8,128)} %get-tuple-element.25.refs_1_, s32[2,8]{1,0:T(2,128)} %pad_add_fusion.refs_2_, s32[8,16]{1,0:T(8,128)} %constant.173.clone.refs_3_, f32[128,8,1024]{2,1,0:T(8,128)} %backward.2.refs_4_, ...), custom_call_target="tpu_custom_call" | custom-call | tf_op jit(solution)/shard_map/backward/pallas_call | solution.py:377
  336.7 0.0 copy-done
  336.7 0.6 broadcast_in_dim_reshape.3
  (7 shorter events, 0.1 us)
Async XLA Ops:
  285.4 51.3 %copy-start = (f32[48,128]{1,0:T(8,128)S(1)}, f32[48,128]{1,0:T(8,128)}, u32[]{:S(2)}) copy-start(f32[48,128]{1,0:T(8,128)} %get-tuple-element.7) | copy-start | bytes 73732

commit v3 on v2

--- a/solution.py
+++ b/solution.py
@@ -25,8 +25,8 @@
 RAYS = NTILE * RAYS_TILE
 LANES = 128
 PAD = 32
-TALL = RAYS + 2 * PAD
 SPAN = 128
+TALL = RAYS + SPAN
 VMEM_LIMIT = 60 * 1024 * 1024
 
 
@@ -63,18 +63,13 @@
         f_scr[a * R:(a + 1) * R, :] = (bump * bump).astype(jnp.bfloat16)
 
 
-def merge_range(win_ref, a):
-    begin = jnp.maximum(win_ref[0, a] - PAD, 0) // SPAN
-    end = jnp.minimum((win_ref[1, a] + R + PAD) // SPAN + 1, RAYS // SPAN)
-    return begin, end
-
-
 def aligned(x, m):
     return pl.multiple_of(x, m)
 
 
 def forward_kernel(nb, lo_ref, frac_ref, win_ref, first_ref, vol_ref, base_ref, out_ref,
-                   e_scr, f_scr, m_scr, acc):
+                   e_scr, f_even, f_odd, m_scr, acc):
+    f_bufs = (f_even, f_odd)
     step = pl.program_id(0)
 
     @pl.when(step == 0)
@@ -84,23 +79,22 @@
         line = lax.broadcasted_iota(jnp.int32, (LANES, VOX), 0)
         q_of = (v // (BLK_SIDE * SUB)) * (BLK_SIDE // SUB) + (v % BLK_SIDE) // SUB
         m_scr[...] = jnp.where(q_of == line // 8, 1.0, 0.0).astype(jnp.bfloat16)
-        zero = jnp.zeros((64, LANES), jnp.float32)
+        zero = jnp.zeros((SPAN, LANES), jnp.float32)
 
         def clear_angle(a, c):
-            begin, end = merge_range(win_ref, a)
-            begin = begin * (SPAN // 64)
-            end = end * (SPAN // 64) + 1
-
             def clear(i, c):
-                acc[pl.ds(aligned(a * TALL + i * 64, 64), 64), :] = zero
+                @pl.when(win_ref[1, a * (TALL // SPAN) + i] > 0)
+                def _():
+                    acc[pl.ds(aligned(a * TALL + i * SPAN, SPAN), SPAN), :] = zero
                 return c
 
-            return lax.fori_loop(begin, end, clear, c)
+            return lax.fori_loop(0, TALL // SPAN, clear, c)
 
         lax.fori_loop(0, ANG_SUB, clear_angle, 0)
 
-    def one(i, c):
+    for i in range(nb):
         b = step * nb + i
+        f_scr = f_bufs[i % 2]
         make_footprint(e_scr, f_scr, frac_ref, b)
         rounded = vol_ref[i].astype(jnp.bfloat16)
         spreadv = jnp.tile(rounded, (NQ, 1)) * m_scr[...]
@@ -109,9 +103,6 @@
         for a in range(ANG_SUB):
             at = pl.ds(a * TALL + PAD + lo_ref[b, a], R)
             acc[at, :] += part[a * R:(a + 1) * R, :]
-        return c
-
-    lax.fori_loop(0, nb, one, 0, unroll=2)
 
     @pl.when(step == pl.num_programs(0) - 1)
     def _():
@@ -122,28 +113,29 @@
         pick = lane_q == row_j
 
         def merge_angle(a, c):
-            begin, end = merge_range(win_ref, a)
-
             def merge(i, c):
-                k = i * span
-                total = jnp.zeros((span, LANES), jnp.float32)
-                for q in range(NQ):
-                    src = a * TALL + PAD + k - first_ref[a, q]
-                    total = jnp.where(lane_q == q, acc[pl.ds(src, span), :], total)
-                for s in (64, 32, 16, 8):
-                    total = total + pltpu.roll(total, s, 1)
-                total = jnp.where(pick, total, 0.0)
-                out = jnp.sum(total.reshape(span // 16, 16, LANES), axis=1)
-                out_ref[pl.ds(aligned(a * (RAYS // 16) + i * 8, 8), 8), :] = out
+                @pl.when(win_ref[0, a * (TALL // SPAN) + i] > 0)
+                def _():
+                    k = i * span
+                    total = jnp.zeros((span, LANES), jnp.float32)
+                    for q in range(NQ):
+                        src = a * TALL + PAD + k - first_ref[a, q]
+                        total = jnp.where(lane_q == q, acc[pl.ds(src, span), :], total)
+                    for s in (64, 32, 16, 8):
+                        total = total + pltpu.roll(total, s, 1)
+                    total = jnp.where(pick, total, 0.0)
+                    out = jnp.sum(total.reshape(span // 16, 16, LANES), axis=1)
+                    out_ref[pl.ds(aligned(a * (RAYS // 16) + i * 8, 8), 8), :] = out
                 return c
 
-            return lax.fori_loop(begin, end, merge, c)
+            return lax.fori_loop(0, RAYS // span, merge, c)
 
         lax.fori_loop(0, ANG_SUB, merge_angle, 0)
 
 
 def backward_kernel(nb, lo_ref, frac_ref, win_ref, first_ref, vol_ref, base_ref, res_ref, out_ref,
-                    e_scr, f_scr, rb, dd):
+                    e_scr, f_even, f_odd, rb, dd):
+    f_bufs = (f_even, f_odd)
     step = pl.program_id(0)
 
     @pl.when(step == 0)
@@ -158,31 +150,30 @@
             == lax.broadcasted_iota(jnp.int32, (LANES, LANES), 1) % 8, 1.0, 0.0).astype(jnp.bfloat16)
 
         def one_angle(a, c):
-            begin = jnp.maximum((win_ref[0, a] - 64) // span, 0)
-            end = jnp.minimum((win_ref[1, a] + 64 + span) // span + 1, RAYS // span)
-
             def widen(i, c):
-                rows = res_ref[pl.ds(aligned(a * (RAYS // 16) + i * 8, 8), 8), :]
-                wide = jnp.broadcast_to(rows[:, None, :], (8, 16, LANES)).reshape(span, LANES)
-                wide = jnp.where(pick, wide, 0.0).astype(jnp.bfloat16)
-                rb[pl.ds(aligned(PAD + i * span, 8), span), :] = jnp.dot(
-                    wide, fold, preferred_element_type=jnp.float32)
+                @pl.when(win_ref[0, a * (TALL // SPAN) + i] > 0)
+                def _():
+                    rows = res_ref[pl.ds(aligned(a * (RAYS // 16) + i * 8, 8), 8), :]
+                    wide = jnp.broadcast_to(rows[:, None, :], (8, 16, LANES)).reshape(span, LANES)
+                    wide = jnp.where(pick, wide, 0.0).astype(jnp.bfloat16)
+                    rb[pl.ds(aligned(PAD + i * span, 8), span), :] = jnp.dot(
+                        wide, fold, preferred_element_type=jnp.float32)
                 return c
 
-            lax.fori_loop(begin, end, widen, 0)
-            first = jnp.maximum(win_ref[0, a] // span, 0)
-            last = jnp.minimum((win_ref[1, a] + 16) // span + 1, RAYS // span)
+            lax.fori_loop(0, RAYS // span, widen, 0)
 
             def shift(i, c):
-                k = i * span
-                total = jnp.zeros((span, LANES), jnp.float32)
-                for q in range(NQ):
-                    src = PAD + k + first_ref[a, q]
-                    total = jnp.where(lane_q == q, rb[pl.ds(src, span), :], total)
-                dd[pl.ds(aligned(a * RAYS + k, span), span), :] = total
+                @pl.when(win_ref[0, a * (TALL // SPAN) + i] > 0)
+                def _():
+                    k = i * span
+                    total = jnp.zeros((span, LANES), jnp.float32)
+                    for q in range(NQ):
+                        src = PAD + k + first_ref[a, q]
+                        total = jnp.where(lane_q == q, rb[pl.ds(src, span), :], total)
+                    dd[pl.ds(aligned(a * RAYS + k, span), span), :] = total
                 return c
 
-            lax.fori_loop(first, last, shift, 0)
+            lax.fori_loop(0, RAYS // span, shift, 0)
             return c
 
         lax.fori_loop(0, ANG_SUB, one_angle, 0)
@@ -192,8 +183,9 @@
     lane = lax.broadcasted_iota(jnp.int32, (8, width), 1)
     col_group = (lane % BLK_SIDE) // SUB
 
-    def one(i, c):
+    for i in range(nb):
         b = step * nb + i
+        f_scr = f_bufs[i % 2]
         make_footprint(e_scr, f_scr, frac_ref, b)
         rows = jnp.concatenate(
             [dd[pl.ds(a * RAYS + lo_ref[b, a], R), :] for a in range(ANG_SUB)], axis=0)
@@ -208,9 +200,6 @@
                 back = jnp.where(col_group == j, part[j * 8:(j + 1) * 8], back)
             col_sum = part[32:40]
             out_ref[i, :, at] = jnp.maximum(vol_ref[i, :, at] + relax * back / col_sum, 0.0)
-        return c
-
-    lax.fori_loop(0, nb, one, 0, unroll=2)
 
 
 def ray_sum_kernel(c_ref, s_ref, k_ref, out_ref):
@@ -225,12 +214,11 @@
         def row(i, total):
             y = i.astype(jnp.float32) + (0.5 - half)
             w = ray - y * sn
-            mid = jnp.floor(w * inv) + 0.5
+            mid = jnp.clip(jnp.floor(w * inv) + 0.5, 2.5 - half, half - 2.5)
             t0 = mid * cs - w
-            for j in range(-2, 3):
-                t = t0 + j * cs
+            for t in (t0 - 2 * cs, t0 - cs, t0, t0 + cs, t0 + 2 * cs):
                 bump = jnp.maximum(1.0 - t * t, 0.0)
-                total = total + jnp.where(jnp.abs(mid + j) < half, bump * bump, 0.0)
+                total = total + bump * bump
             return total
 
         out_ref[u] = lax.fori_loop(0, side, row, jnp.zeros(out_ref.shape[1:], jnp.float32), unroll=8)
@@ -364,6 +352,7 @@
         out_shape=jax.ShapeDtypeStruct((lines, LANES), jnp.float32),
         scratch_shapes=[pltpu.VMEM((ANG_SUB * R, VOX), jnp.float32),
                         pltpu.VMEM((ANG_SUB * R, VOX), jnp.bfloat16),
+                        pltpu.VMEM((ANG_SUB * R, VOX), jnp.bfloat16),
                         pltpu.VMEM((LANES, VOX), jnp.bfloat16),
                         pltpu.VMEM((ANG_SUB * TALL, LANES), jnp.float32)],
         compiler_params=pltpu.CompilerParams(vmem_limit_bytes=VMEM_LIMIT),
@@ -384,6 +373,7 @@
         out_specs=pl.BlockSpec((nb, slices, VOX), lambda i: (i, 0, 0)),
         out_shape=jax.ShapeDtypeStruct(volume.shape, jnp.float32),
         scratch_shapes=[pltpu.VMEM((ANG_SUB * R, VOX), jnp.float32),
+                        pltpu.VMEM((ANG_SUB * R, VOX), jnp.bfloat16),
                         pltpu.VMEM((ANG_SUB * R, VOX), jnp.bfloat16),
                         pltpu.VMEM((TALL, LANES), jnp.float32),
                         pltpu.VMEM((ANG_SUB * RAYS, LANES), jnp.float32)],
@@ -431,7 +421,11 @@
     z = x[:, None] * cosine + y[:, None] * sine + (RAYS * 0.5 - 0.5)
     low = jnp.floor(z)
     lo = low.astype(jnp.int32)
-    win = jnp.stack([jnp.min(lo, axis=0), jnp.max(lo, axis=0)])
+    tile = jnp.arange(TALL // SPAN, dtype=jnp.int32)
+    touched = jnp.any(((lo - PAD) // SPAN)[:, :, None] == tile, axis=0)
+    touched |= jnp.any(((lo + R + PAD) // SPAN)[:, :, None] == tile, axis=0)
+    cleared = touched | jnp.pad(touched[:, :-1], ((0, 0), (1, 0)))
+    win = jnp.stack([touched.reshape(-1), cleared.reshape(-1)]).astype(jnp.int32)
     return lo, (z - low) * (1.0 / spread), win
 
 

time: 339 us -> 277 us (0.82)
  the two profiles are of different devices: /device:TPU:9 before, /device:TPU:0 now
where the time goes in v3:
time: 277 us; the launch traced here: 273 us
  Pallas kernels  255 us (92%)
  local copies, waits for them, and re-layouts  9.45 us (3%)
  other arithmetic  7.82 us (3%)
    pallas_call x2, Pallas kernels, forward(): pl.pallas_call(lambda *refs: forward_kernel(nb, *refs), grid=(blocks // n...  88.9 us
    pallas_call x2, Pallas kernels, backward(): pl.pallas_call(lambda *refs: backward_kernel(nb, *refs), grid=(blocks //...  68.4 us
    pallas_call x2, Pallas kernels, exchange(): pl.pallas_call(exchange_kernel, in_specs=[vmem] * 4, out_specs=[vmem] * 2...  67.4 us
    pallas_call x1, Pallas kernels, own_ray_sums(): pl.pallas_call(ray_sum_kernel, out_shape=jax.ShapeDtypeStruct(shape, jnp....  30.7 us

profile of v3, /device:TPU:0, one launch (start us, length us, event | category | flops | bytes accessed | tf_op | source)
XLA Modules:
  0.0 273.3 jit_solution(11014487870441166501)
XLA Ops:
  0.6 0.7 fusion.37
  1.3 0.6 broadcast_in_dim.129.k_ref
  1.9 0.8 fusion.39
  2.7 0.1 fusion.33
  2.8 0.1 fusion.14
  2.8 0.1 fusion.15
  3.0 0.6 pad_maximum_fusion.1.s_ref
  3.6 0.6 pad_maximum_fusion.c_ref
  4.2 30.7 %raysum.1 = f32[2,8,128]{2,1,0:T(8,128)} custom-call(f32[2,8,128]{2,1,0:T(8,128)} %pad_maximum_fusion.c_ref, f32[2,8,128]{2,1,0:T(8,128)} %pad_maximum_fusion.1.s_ref, f32[2,8,128]{2,1,0:T(8,128)} %broadcast_in_dim.129.k_ref), custom_call_target="tpu_custom_call" | custom-call | tf_op jit(solution)/shard_map/raysum/pallas_call | solution.py:407
  34.9 0.7 copy.32
  35.6 0.1 max.23
  35.7 0.1 copy.28
  35.8 0.1 max.21
  35.8 0.1 copy.26
  35.9 0.7 copy.27.rs_ref
  36.6 0.7 copy.29.rs_ref
  37.3 1.0 fusion.38
  38.3 0.6 reshape.648.mine_ref
  38.9 0.6 reshape.643.mine_ref
  39.5 1.5 fusion.5
  41.0 1.0 add_select_fusion
  42.1 0.1 copy.22
  42.1 1.0 fusion.2
  43.1 0.1 copy.24
  43.2 0.1 or.40
  43.3 0.1 copy.25
  43.4 0.1 stack_reshape.9
  43.5 0.6 add_convert_fusion.1.refs_2_
  44.1 0.1 copy.19
  44.2 1.0 fusion
  45.2 0.1 copy.20
  45.3 0.1 or.37
  45.4 0.1 copy.21
  45.5 0.1 stack_reshape.8
  45.6 0.6 add_convert_fusion.refs_2_
  46.2 0.2 broadcast_in_dim.131
  46.3 0.8 convert_element_type.50.on_ref
  47.1 0.2 broadcast_in_dim.112
  47.3 0.8 convert_element_type.47.on_ref
  48.1 44.7 %forward.2 = f32[1536,128]{1,0:T(8,128)} custom-call(s32[128,8]{1,0:T(8,128)} %get-tuple-element.17.refs_0_, f32[128,8]{1,0:T(8,128)} %get-tuple-element.16.refs_1_, s32[2,200]{1,0:T(2,128)} %add_convert_fusion.1.refs_2_, s32[8,16]{1,0:T(8,128)} %constant.211.clone.refs_3_, f32[128,8,1024]{2,1,0:T(8,128)} %refs_4_.3, f32[8,1024]{1,0:T(8,128)} %constant.212.clone.refs_5_), custom_call_target="tpu_custom_call" | custom-call | tf_op jit(solution)/shard_map/forward/pallas_call | solution.py:345
  92.8 32.4 %exchange.2 = (f32[4,2,4,48,128]{4,3,2,1,0:T(8,128)}, f32[48,128]{1,0:T(8,128)}) custom-call(f32[4,2,4,48,128]{4,3,2,1,0:T(8,128)} %bitcast.16, f32[48,128]{1,0:T(8,128)} %reshape.643.mine_ref, f32[48,128]{1,0:T(8,128)} %convert_element_type.47.on_ref, f32[48,128]{1,0:T(8,128)} %copy.27.rs_ref), custom_call_target="tpu_custom_call" | custom-call | tf_op jit(solution)/shard_map/exchange/pallas_call | solution.py:319
  125.2 34.4 %backward.2.refs_4_ = f32[128,8,1024]{2,1,0:T(8,128)} custom-call(s32[128,8]{1,0:T(8,128)} %get-tuple-element.17.refs_0_, f32[128,8]{1,0:T(8,128)} %get-tuple-element.16.refs_1_, s32[2,200]{1,0:T(2,128)} %add_convert_fusion.1.refs_2_, s32[8,16]{1,0:T(8,128)} %constant.211.clone.refs_3_, f32[128,8,1024]{2,1,0:T(8,128)} %refs_4_.3, ...), custom_call_target="tpu_custom_call" | custom-call | tf_op jit(solution)/shard_map/backward/pallas_call | solution.py:366
  159.6 44.1 %forward.3 = f32[1536,128]{1,0:T(8,128)} custom-call(s32[128,8]{1,0:T(8,128)} %get-tuple-element.24.refs_0_, f32[128,8]{1,0:T(8,128)} %get-tuple-element.25.refs_1_, s32[2,200]{1,0:T(2,128)} %add_convert_fusion.refs_2_, s32[8,16]{1,0:T(8,128)} %constant.215.clone.refs_3_, f32[128,8,1024]{2,1,0:T(8,128)} %backward.2.refs_4_, f32[8,1024]{1,0:T(8,128)} %constant.216.clone.refs_5_), custom_call_target="tpu_custom_call" | custom-call | tf_op jit(solution)/shard_map/forward/pallas_call | solution.py:345
  203.8 35.0 %exchange.3 = (f32[4,2,4,48,128]{4,3,2,1,0:T(8,128)}, f32[48,128]{1,0:T(8,128)}) custom-call(f32[4,2,4,48,128]{4,3,2,1,0:T(8,128)} %bitcast.17, f32[48,128]{1,0:T(8,128)} %reshape.648.mine_ref, f32[48,128]{1,0:T(8,128)} %convert_element_type.50.on_ref, f32[48,128]{1,0:T(8,128)} %copy.29.rs_ref), custom_call_target="tpu_custom_call" | custom-call | tf_op jit(solution)/shard_map/exchange/pallas_call | solution.py:319
  238.7 0.0 copy-start
  238.8 34.0 %backward.3 = f32[128,8,1024]{2,1,0:T(8,128)} custom-call(s32[128,8]{1,0:T(8,128)} %get-tuple-element.24.refs_0_, f32[128,8]{1,0:T(8,128)} %get-tuple-element.25.refs_1_, s32[2,200]{1,0:T(2,128)} %add_convert_fusion.refs_2_, s32[8,16]{1,0:T(8,128)} %constant.215.clone.refs_3_, f32[128,8,1024]{2,1,0:T(8,128)} %backward.2.refs_4_, ...), custom_call_target="tpu_custom_call" | custom-call | tf_op jit(solution)/shard_map/backward/pallas_call | solution.py:366
  272.7 0.0 copy-done
  272.7 0.6 broadcast_in_dim_reshape.3
  (15 shorter events, 0.3 us)
Async XLA Ops:
  238.7 34.0 %copy-start = (f32[48,128]{1,0:T(8,128)S(1)}, f32[48,128]{1,0:T(8,128)}, u32[]{:S(2)}) copy-start(f32[48,128]{1,0:T(8,128)} %get-tuple-element.7) | copy-start | bytes 73732

commit v4 on v3

--- a/solution.py
+++ b/solution.py
@@ -67,9 +67,8 @@
     return pl.multiple_of(x, m)
 
 
-def forward_kernel(nb, lo_ref, frac_ref, win_ref, first_ref, vol_ref, base_ref, out_ref,
-                   e_scr, f_even, f_odd, m_scr, acc):
-    f_bufs = (f_even, f_odd)
+def forward_kernel(nb, lo_ref, frac_ref, win_ref, first_ref, vol_ref, base_ref, out_ref, foot_ref,
+                   e_scr, m_scr, acc):
     step = pl.program_id(0)
 
     @pl.when(step == 0)
@@ -94,11 +93,10 @@
 
     for i in range(nb):
         b = step * nb + i
-        f_scr = f_bufs[i % 2]
-        make_footprint(e_scr, f_scr, frac_ref, b)
+        make_footprint(e_scr, foot_ref.at[i], frac_ref, b)
         rounded = vol_ref[i].astype(jnp.bfloat16)
         spreadv = jnp.tile(rounded, (NQ, 1)) * m_scr[...]
-        part = lax.dot_general(f_scr[...], spreadv, (((1,), (1,)), ((), ())),
+        part = lax.dot_general(foot_ref[i], spreadv, (((1,), (1,)), ((), ())),
                                preferred_element_type=jnp.float32)
         for a in range(ANG_SUB):
             at = pl.ds(a * TALL + PAD + lo_ref[b, a], R)
@@ -133,14 +131,11 @@
         lax.fori_loop(0, ANG_SUB, merge_angle, 0)
 
 
-def backward_kernel(nb, lo_ref, frac_ref, win_ref, first_ref, vol_ref, base_ref, res_ref, out_ref,
-                    e_scr, f_even, f_odd, rb, dd):
-    f_bufs = (f_even, f_odd)
+def backward_kernel(nb, lo_ref, win_ref, first_ref, vol_ref, foot_ref, res_ref, out_ref, rb, dd):
     step = pl.program_id(0)
 
     @pl.when(step == 0)
     def _():
-        fill_grid(base_ref, e_scr)
         span = SPAN
         lane_q = lax.broadcasted_iota(jnp.int32, (span, LANES), 1) // 8
         row_j = lax.broadcasted_iota(jnp.int32, (span, LANES), 0) % 16
@@ -185,8 +180,6 @@
 
     for i in range(nb):
         b = step * nb + i
-        f_scr = f_bufs[i % 2]
-        make_footprint(e_scr, f_scr, frac_ref, b)
         rows = jnp.concatenate(
             [dd[pl.ds(a * RAYS + lo_ref[b, a], R), :] for a in range(ANG_SUB)], axis=0)
         turned = jnp.transpose(rows)
@@ -194,7 +187,7 @@
         for g in range(group):
             lhs = jnp.concatenate([turned[g * 32:(g + 1) * 32], ones], axis=0).astype(jnp.bfloat16)
             at = slice(g * width, (g + 1) * width)
-            part = jnp.dot(lhs, f_scr[:, at], preferred_element_type=jnp.float32)
+            part = jnp.dot(lhs, foot_ref[i, :, at], preferred_element_type=jnp.float32)
             back = part[0:8]
             for j in range(1, group):
                 back = jnp.where(col_group == j, part[j * 8:(j + 1) * 8], back)
@@ -348,11 +341,11 @@
         in_specs=[smem(), smem(), smem(), smem(),
                   pl.BlockSpec((nb, slices, VOX), lambda i: (i, 0, 0)),
                   pl.BlockSpec((ANG_SUB, VOX), lambda i: (0, 0))],
-        out_specs=pl.BlockSpec((lines, LANES), lambda i: (0, 0)),
-        out_shape=jax.ShapeDtypeStruct((lines, LANES), jnp.float32),
+        out_specs=[pl.BlockSpec((lines, LANES), lambda i: (0, 0)),
+                   pl.BlockSpec((nb, ANG_SUB * R, VOX), lambda i: (i, 0, 0))],
+        out_shape=[jax.ShapeDtypeStruct((lines, LANES), jnp.float32),
+                   jax.ShapeDtypeStruct((blocks, ANG_SUB * R, VOX), jnp.bfloat16)],
         scratch_shapes=[pltpu.VMEM((ANG_SUB * R, VOX), jnp.float32),
-                        pltpu.VMEM((ANG_SUB * R, VOX), jnp.bfloat16),
-                        pltpu.VMEM((ANG_SUB * R, VOX), jnp.bfloat16),
                         pltpu.VMEM((LANES, VOX), jnp.bfloat16),
                         pltpu.VMEM((ANG_SUB * TALL, LANES), jnp.float32)],
         compiler_params=pltpu.CompilerParams(vmem_limit_bytes=VMEM_LIMIT),
@@ -360,26 +353,23 @@
     )(lo, frac, win, first, volume, base)
 
 
-def backward(volume, residual, lo, frac, win, base, first):
+def backward(volume, residual, lo, win, foot, first):
     blocks, slices, _ = volume.shape
     nb = 8
     return pl.pallas_call(
         lambda *refs: backward_kernel(nb, *refs),
         grid=(blocks // nb,),
-        in_specs=[smem(), smem(), smem(), smem(),
+        in_specs=[smem(), smem(), smem(),
                   pl.BlockSpec((nb, slices, VOX), lambda i: (i, 0, 0)),
-                  pl.BlockSpec((ANG_SUB, VOX), lambda i: (0, 0)),
+                  pl.BlockSpec((nb, ANG_SUB * R, VOX), lambda i: (i, 0, 0)),
                   pl.BlockSpec(residual.shape, lambda i: (0, 0))],
         out_specs=pl.BlockSpec((nb, slices, VOX), lambda i: (i, 0, 0)),
         out_shape=jax.ShapeDtypeStruct(volume.shape, jnp.float32),
-        scratch_shapes=[pltpu.VMEM((ANG_SUB * R, VOX), jnp.float32),
-                        pltpu.VMEM((ANG_SUB * R, VOX), jnp.bfloat16),
-                        pltpu.VMEM((ANG_SUB * R, VOX), jnp.bfloat16),
-                        pltpu.VMEM((TALL, LANES), jnp.float32),
+        scratch_shapes=[pltpu.VMEM((TALL, LANES), jnp.float32),
                         pltpu.VMEM((ANG_SUB * RAYS, LANES), jnp.float32)],
         compiler_params=pltpu.CompilerParams(vmem_limit_bytes=VMEM_LIMIT),
         name="backward",
-    )(lo, frac, win, first, volume, base, residual)
+    )(lo, win, first, volume, foot, residual)
 
 
 def own_ray_sums(first_row, rows):
@@ -446,7 +436,7 @@
     for subset in range(SUBSETS):
         base, first = geometry(subset)
         lo, frac, win = placing(block_place, subset)
-        partial = forward(estimate, lo, frac, win, base, first)
+        partial, foot = forward(estimate, lo, frac, win, base, first)
         mine = lax.dynamic_slice_in_dim(measured[subset], group_index * rows, rows, 0)
         live = lax.dynamic_slice_in_dim(live_rays[subset], first_row, rows, 0)
         on = jnp.arange(RAYS_TILE, dtype=jnp.int32)[None, :] < live[:, None]
@@ -455,7 +445,7 @@
         rs = jnp.broadcast_to(rs, (lines, per, slices)).reshape(lines, LANES)
         full, own = exchange(partial, mine.reshape(lines, LANES), on.astype(jnp.float32), rs, groups, patches)
         own_residual = own.reshape(rows, RAYS_TILE * slices)
-        estimate = backward(estimate, full, lo, frac, win, base, first)
+        estimate = backward(estimate, full, lo, win, foot, first)
     return (estimate, own_residual[None])
 
 

time: 277 us -> 283 us (1.022)
  Pallas kernels: 255 us -> 262 us
    pallas_call x2, Pallas kernels: 88.9 us -> 96.4 us  [forward(): pl.pallas_call(lambda *refs: forward_kernel(nb, *refs), grid=(blocks // n...]
    pallas_call x2, Pallas kernels: 67.4 us -> 63.4 us  [exchange(): pl.pallas_call(exchange_kernel, in_specs=[vmem] * 4, out_specs=[vmem] * 2...]
    pallas_call x2, Pallas kernels: 68.4 us -> 71.8 us  [backward(): pl.pallas_call(lambda *refs: backward_kernel(nb, *refs), grid=(blocks //...]
where the time goes in v4:
time: 283 us; the launch traced here: 280 us
  Pallas kernels  262 us (93%)
  local copies, waits for them, and re-layouts  9.46 us (3%)
  other arithmetic  7.81 us (3%)
    pallas_call x2, Pallas kernels, forward(): pl.pallas_call(lambda *refs: forward_kernel(nb, *refs), grid=(blocks // n...  96.4 us
    pallas_call x2, Pallas kernels, backward(): pl.pallas_call(lambda *refs: backward_kernel(nb, *refs), grid=(blocks //...  71.8 us
    pallas_call x2, Pallas kernels, exchange(): pl.pallas_call(exchange_kernel, in_specs=[vmem] * 4, out_specs=[vmem] * 2...  63.4 us
    pallas_call x1, Pallas kernels, own_ray_sums(): pl.pallas_call(ray_sum_kernel, out_shape=jax.ShapeDtypeStruct(shape, jnp....  30.7 us

profile of v4, /device:TPU:0, one launch (start us, length us, event | category | flops | bytes accessed | tf_op | source)
XLA Modules:
  0.0 280.4 jit_solution(17893473681381231889)
XLA Ops:
  0.6 0.7 fusion.37
  1.3 0.6 broadcast_in_dim.129.k_ref
  1.9 0.8 fusion.39
  2.7 0.1 fusion.33
  2.8 0.1 fusion.14
  2.8 0.1 fusion.15
  3.0 0.6 pad_maximum_fusion.1.s_ref
  3.6 0.6 pad_maximum_fusion.c_ref
  4.2 30.7 %raysum.1 = f32[2,8,128]{2,1,0:T(8,128)} custom-call(f32[2,8,128]{2,1,0:T(8,128)} %pad_maximum_fusion.c_ref, f32[2,8,128]{2,1,0:T(8,128)} %pad_maximum_fusion.1.s_ref, f32[2,8,128]{2,1,0:T(8,128)} %broadcast_in_dim.129.k_ref), custom_call_target="tpu_custom_call" | custom-call | tf_op jit(solution)/shard_map/raysum/pallas_call | solution.py:397
  34.9 0.7 copy.32
  35.6 0.1 max.23
  35.7 0.1 copy.28
  35.8 0.1 max.21
  35.8 0.1 copy.26
  35.9 0.7 copy.27.rs_ref
  36.6 0.7 copy.29.rs_ref
  37.3 1.0 fusion.38
  38.3 0.6 reshape.648.mine_ref
  38.9 0.6 reshape.643.mine_ref
  39.5 1.5 fusion.4
  41.0 1.0 add_select_fusion
  42.0 0.1 copy.22
  42.1 1.0 fusion.2
  43.1 0.1 copy.24
  43.2 0.1 or.40
  43.3 0.1 copy.25
  43.4 0.1 stack_reshape.9
  43.5 0.6 add_convert_fusion.1.refs_2_.refs_1_
  44.1 0.1 copy.19
  44.2 1.0 fusion
  45.2 0.1 copy.20
  45.3 0.1 or.37
  45.4 0.1 copy.21
  45.5 0.1 stack_reshape.8
  45.6 0.6 add_convert_fusion.refs_2_.refs_1_
  46.2 0.2 broadcast_in_dim.131
  46.3 0.8 convert_element_type.50.on_ref
  47.1 0.2 broadcast_in_dim.112
  47.3 0.8 convert_element_type.47.on_ref
  48.1 48.3 %forward.2 = (f32[1536,128]{1,0:T(8,128)}, bf16[128,128,1024]{2,1,0:T(8,128)(2,1)}) custom-call(s32[128,8]{1,0:T(8,128)} %get-tuple-element.30.refs_0_, f32[128,8]{1,0:T(8,128)} %get-tuple-element.31.refs_1_, s32[2,200]{1,0:T(2,128)} %add_convert_fusion.1.refs_2_.refs_1_, s32[8,16]{1,0:T(8,128)} %constant.211.clone.refs_3_.refs_2_, f32[128,8,1024]{2,1,0:T(8,128)} %refs_3_.3, ...), custom_call_target="tpu_custom_call" | custom-call | tf_op jit(solution)/shard_map/forward/pallas_call | solution.py:338
  96.4 31.6 %exchange.2 = (f32[4,2,4,48,128]{4,3,2,1,0:T(8,128)}, f32[48,128]{1,0:T(8,128)}) custom-call(f32[4,2,4,48,128]{4,3,2,1,0:T(8,128)} %bitcast.16, f32[48,128]{1,0:T(8,128)} %reshape.643.mine_ref, f32[48,128]{1,0:T(8,128)} %convert_element_type.47.on_ref, f32[48,128]{1,0:T(8,128)} %copy.27.rs_ref), custom_call_target="tpu_custom_call" | custom-call | tf_op jit(solution)/shard_map/exchange/pallas_call | solution.py:312
  128.0 36.0 %backward.2.refs_4_.refs_3_ = f32[128,8,1024]{2,1,0:T(8,128)} custom-call(s32[128,8]{1,0:T(8,128)} %get-tuple-element.30.refs_0_, s32[2,200]{1,0:T(2,128)} %add_convert_fusion.1.refs_2_.refs_1_, s32[8,16]{1,0:T(8,128)} %constant.211.clone.refs_3_.refs_2_, f32[128,8,1024]{2,1,0:T(8,128)} %refs_3_.3, bf16[128,128,1024]{2,1,0:T(8,128)(2,1)} %get-tuple-element.9.refs_4_, ...), custom_call_target="tpu_custom_call" | custom-call | tf_op jit(solution)/shard_map/backward/pallas_call | solution.py:359
  163.9 48.1 %forward.3 = (f32[1536,128]{1,0:T(8,128)}, bf16[128,128,1024]{2,1,0:T(8,128)(2,1)}) custom-call(s32[128,8]{1,0:T(8,128)} %get-tuple-element.23.refs_0_, f32[128,8]{1,0:T(8,128)} %get-tuple-element.22.refs_1_, s32[2,200]{1,0:T(2,128)} %add_convert_fusion.refs_2_.refs_1_, s32[8,16]{1,0:T(8,128)} %constant.215.clone.refs_3_.refs_2_, ...), custom_call_target="tpu_custom_call" | custom-call | tf_op jit(solution)/shard_map/forward/pallas_call | solution.py:338
  212.1 31.9 %exchange.3 = (f32[4,2,4,48,128]{4,3,2,1,0:T(8,128)}, f32[48,128]{1,0:T(8,128)}) custom-call(f32[4,2,4,48,128]{4,3,2,1,0:T(8,128)} %bitcast.17, f32[48,128]{1,0:T(8,128)} %reshape.648.mine_ref, f32[48,128]{1,0:T(8,128)} %convert_element_type.50.on_ref, f32[48,128]{1,0:T(8,128)} %copy.29.rs_ref), custom_call_target="tpu_custom_call" | custom-call | tf_op jit(solution)/shard_map/exchange/pallas_call | solution.py:312
  243.9 0.0 copy-start
  243.9 35.8 %backward.3 = f32[128,8,1024]{2,1,0:T(8,128)} custom-call(s32[128,8]{1,0:T(8,128)} %get-tuple-element.23.refs_0_, s32[2,200]{1,0:T(2,128)} %add_convert_fusion.refs_2_.refs_1_, s32[8,16]{1,0:T(8,128)} %constant.215.clone.refs_3_.refs_2_, f32[128,8,1024]{2,1,0:T(8,128)} %backward.2.refs_4_.refs_3_, bf16[128,128,1024]{2,1,0:T(8,128)(2,1)} %get-tuple-element.12.refs_4_, ...), custom_call_target="tpu_custom_call" | custom-call | tf_op jit(solution)/shard_map/backward/pallas_call | solution.py:359
  279.8 0.0 copy-done
  279.8 0.6 broadcast_in_dim_reshape.3
  (15 shorter events, 0.3 us)
Async XLA Ops:
  243.9 35.8 %copy-start = (f32[48,128]{1,0:T(8,128)S(1)}, f32[48,128]{1,0:T(8,128)}, u32[]{:S(2)}) copy-start(f32[48,128]{1,0:T(8,128)} %get-tuple-element.15) | copy-start | bytes 73732

commit v5 on v3

--- a/solution.py
+++ b/solution.py
@@ -63,12 +63,36 @@
         f_scr[a * R:(a + 1) * R, :] = (bump * bump).astype(jnp.bfloat16)
 
 
+TILES = RAYS // SPAN
+
+
+def list_tiles(win_ref, tiles):
+    def step(i, n):
+        hit = win_ref[i]
+        tiles[n] = i
+        return n + hit
+
+    n = lax.fori_loop(0, ANG_SUB * TILES, step, 0)
+    tiles[n] = tiles[jnp.maximum(n - 1, 0)]
+    return (n + 1) // 2
+
+
+def over_tiles(tiles, half_count, body):
+    def pair(i, c):
+        for j in range(2):
+            at = tiles[2 * i + j]
+            body(at // TILES, lax.rem(at, TILES))
+        return c
+
+    lax.fori_loop(0, half_count, pair, 0)
+
+
 def aligned(x, m):
     return pl.multiple_of(x, m)
 
 
 def forward_kernel(nb, lo_ref, frac_ref, win_ref, first_ref, vol_ref, base_ref, out_ref,
-                   e_scr, f_even, f_odd, m_scr, acc):
+                   e_scr, f_even, f_odd, m_scr, acc, tiles):
     f_bufs = (f_even, f_odd)
     step = pl.program_id(0)
 
@@ -79,18 +103,14 @@
         line = lax.broadcasted_iota(jnp.int32, (LANES, VOX), 0)
         q_of = (v // (BLK_SIDE * SUB)) * (BLK_SIDE // SUB) + (v % BLK_SIDE) // SUB
         m_scr[...] = jnp.where(q_of == line // 8, 1.0, 0.0).astype(jnp.bfloat16)
-        zero = jnp.zeros((SPAN, LANES), jnp.float32)
-
-        def clear_angle(a, c):
-            def clear(i, c):
-                @pl.when(win_ref[1, a * (TALL // SPAN) + i] > 0)
-                def _():
-                    acc[pl.ds(aligned(a * TALL + i * SPAN, SPAN), SPAN), :] = zero
-                return c
-
-            return lax.fori_loop(0, TALL // SPAN, clear, c)
-
-        lax.fori_loop(0, ANG_SUB, clear_angle, 0)
+        zero = jnp.zeros((2 * SPAN, LANES), jnp.float32)
+
+        tiles[ANG_SUB * TILES + 1] = list_tiles(win_ref, tiles)
+
+        def clear(a, i):
+            acc[pl.ds(aligned(a * TALL + i * SPAN, SPAN), 2 * SPAN), :] = zero
+
+        over_tiles(tiles, tiles[ANG_SUB * TILES + 1], clear)
 
     for i in range(nb):
         b = step * nb + i
@@ -112,29 +132,23 @@
         row_j = lax.broadcasted_iota(jnp.int32, (span, LANES), 0) % 16
         pick = lane_q == row_j
 
-        def merge_angle(a, c):
-            def merge(i, c):
-                @pl.when(win_ref[0, a * (TALL // SPAN) + i] > 0)
-                def _():
-                    k = i * span
-                    total = jnp.zeros((span, LANES), jnp.float32)
-                    for q in range(NQ):
-                        src = a * TALL + PAD + k - first_ref[a, q]
-                        total = jnp.where(lane_q == q, acc[pl.ds(src, span), :], total)
-                    for s in (64, 32, 16, 8):
-                        total = total + pltpu.roll(total, s, 1)
-                    total = jnp.where(pick, total, 0.0)
-                    out = jnp.sum(total.reshape(span // 16, 16, LANES), axis=1)
-                    out_ref[pl.ds(aligned(a * (RAYS // 16) + i * 8, 8), 8), :] = out
-                return c
-
-            return lax.fori_loop(0, RAYS // span, merge, c)
-
-        lax.fori_loop(0, ANG_SUB, merge_angle, 0)
+        def merge(a, i):
+            k = i * span
+            total = jnp.zeros((span, LANES), jnp.float32)
+            for q in range(NQ):
+                src = a * TALL + PAD + k - first_ref[a, q]
+                total = jnp.where(lane_q == q, acc[pl.ds(src, span), :], total)
+            for s in (64, 32, 16, 8):
+                total = total + pltpu.roll(total, s, 1)
+            total = jnp.where(pick, total, 0.0)
+            out = jnp.sum(total.reshape(span // 16, 16, LANES), axis=1)
+            out_ref[pl.ds(aligned(a * (RAYS // 16) + i * 8, 8), 8), :] = out
+
+        over_tiles(tiles, tiles[ANG_SUB * TILES + 1], merge)
 
 
 def backward_kernel(nb, lo_ref, frac_ref, win_ref, first_ref, vol_ref, base_ref, res_ref, out_ref,
-                    e_scr, f_even, f_odd, rb, dd):
+                    e_scr, f_even, f_odd, rb, dd, tiles):
     f_bufs = (f_even, f_odd)
     step = pl.program_id(0)
 
@@ -149,34 +163,25 @@
             lax.broadcasted_iota(jnp.int32, (LANES, LANES), 0) % 8
             == lax.broadcasted_iota(jnp.int32, (LANES, LANES), 1) % 8, 1.0, 0.0).astype(jnp.bfloat16)
 
-        def one_angle(a, c):
-            def widen(i, c):
-                @pl.when(win_ref[0, a * (TALL // SPAN) + i] > 0)
-                def _():
-                    rows = res_ref[pl.ds(aligned(a * (RAYS // 16) + i * 8, 8), 8), :]
-                    wide = jnp.broadcast_to(rows[:, None, :], (8, 16, LANES)).reshape(span, LANES)
-                    wide = jnp.where(pick, wide, 0.0).astype(jnp.bfloat16)
-                    rb[pl.ds(aligned(PAD + i * span, 8), span), :] = jnp.dot(
-                        wide, fold, preferred_element_type=jnp.float32)
-                return c
-
-            lax.fori_loop(0, RAYS // span, widen, 0)
-
-            def shift(i, c):
-                @pl.when(win_ref[0, a * (TALL // SPAN) + i] > 0)
-                def _():
-                    k = i * span
-                    total = jnp.zeros((span, LANES), jnp.float32)
-                    for q in range(NQ):
-                        src = PAD + k + first_ref[a, q]
-                        total = jnp.where(lane_q == q, rb[pl.ds(src, span), :], total)
-                    dd[pl.ds(aligned(a * RAYS + k, span), span), :] = total
-                return c
-
-            lax.fori_loop(0, RAYS // span, shift, 0)
-            return c
-
-        lax.fori_loop(0, ANG_SUB, one_angle, 0)
+        count = list_tiles(win_ref, tiles)
+
+        def widen(a, i):
+            rows = res_ref[pl.ds(aligned(a * (RAYS // 16) + i * 8, 8), 8), :]
+            wide = jnp.broadcast_to(rows[:, None, :], (8, 16, LANES)).reshape(span, LANES)
+            wide = jnp.where(pick, wide, 0.0).astype(jnp.bfloat16)
+            rb[pl.ds(aligned(a * TALL + PAD + i * span, 8), span), :] = jnp.dot(
+                wide, fold, preferred_element_type=jnp.float32)
+
+        def shift(a, i):
+            k = i * span
+            total = jnp.zeros((span, LANES), jnp.float32)
+            for q in range(NQ):
+                src = a * TALL + PAD + k + first_ref[a, q]
+                total = jnp.where(lane_q == q, rb[pl.ds(src, span), :], total)
+            dd[pl.ds(aligned(a * RAYS + k, span), span), :] = total
+
+        over_tiles(tiles, count, widen)
+        over_tiles(tiles, count, shift)
 
     width = SUB * BLK_SIDE
     group = BLK_SIDE // SUB
@@ -354,7 +359,8 @@
                         pltpu.VMEM((ANG_SUB * R, VOX), jnp.bfloat16),
                         pltpu.VMEM((ANG_SUB * R, VOX), jnp.bfloat16),
                         pltpu.VMEM((LANES, VOX), jnp.bfloat16),
-                        pltpu.VMEM((ANG_SUB * TALL, LANES), jnp.float32)],
+                        pltpu.VMEM((ANG_SUB * TALL, LANES), jnp.float32),
+                        pltpu.SMEM((ANG_SUB * TILES + 2,), jnp.int32)],
         compiler_params=pltpu.CompilerParams(vmem_limit_bytes=VMEM_LIMIT),
         name="forward",
     )(lo, frac, win, first, volume, base)
@@ -375,8 +381,9 @@
         scratch_shapes=[pltpu.VMEM((ANG_SUB * R, VOX), jnp.float32),
                         pltpu.VMEM((ANG_SUB * R, VOX), jnp.bfloat16),
                         pltpu.VMEM((ANG_SUB * R, VOX), jnp.bfloat16),
-                        pltpu.VMEM((TALL, LANES), jnp.float32),
-                        pltpu.VMEM((ANG_SUB * RAYS, LANES), jnp.float32)],
+                        pltpu.VMEM((ANG_SUB * TALL, LANES), jnp.float32),
+                        pltpu.VMEM((ANG_SUB * RAYS, LANES), jnp.float32),
+                        pltpu.SMEM((ANG_SUB * TILES + 2,), jnp.int32)],
         compiler_params=pltpu.CompilerParams(vmem_limit_bytes=VMEM_LIMIT),
         name="backward",
     )(lo, frac, win, first, volume, base, residual)
@@ -421,11 +428,10 @@
     z = x[:, None] * cosine + y[:, None] * sine + (RAYS * 0.5 - 0.5)
     low = jnp.floor(z)
     lo = low.astype(jnp.int32)
-    tile = jnp.arange(TALL // SPAN, dtype=jnp.int32)
+    tile = jnp.arange(TILES, dtype=jnp.int32)
     touched = jnp.any(((lo - PAD) // SPAN)[:, :, None] == tile, axis=0)
     touched |= jnp.any(((lo + R + PAD) // SPAN)[:, :, None] == tile, axis=0)
-    cleared = touched | jnp.pad(touched[:, :-1], ((0, 0), (1, 0)))
-    win = jnp.stack([touched.reshape(-1), cleared.reshape(-1)]).astype(jnp.int32)
+    win = touched.reshape(-1).astype(jnp.int32)
     return lo, (z - low) * (1.0 / spread), win
 
 

time: 277 us -> 241 us (0.87)
  Pallas kernels: 255 us -> 223 us
    pallas_call x2, Pallas kernels: 88.9 us -> 70.9 us  [forward(): pl.pallas_call(lambda *refs: forward_kernel(nb, *refs), grid=(blocks // n...]
    pallas_call x2, Pallas kernels: 68.4 us -> 58.6 us  [backward(): pl.pallas_call(lambda *refs: backward_kernel(nb, *refs), grid=(blocks //...]
    pallas_call x2, Pallas kernels: 67.4 us -> 62.8 us  [exchange(): pl.pallas_call(exchange_kernel, in_specs=[vmem] * 4, out_specs=[vmem] * 2...]
where the time goes in v5:
time: 241 us; the launch traced here: 239 us
  Pallas kernels  223 us (93%)
  local copies, waits for them, and re-layouts  10.1 us (4%)
  other arithmetic  5.41 us (2%)
    pallas_call x2, Pallas kernels, forward(): pl.pallas_call(lambda *refs: forward_kernel(nb, *refs), grid=(blocks // n...  70.9 us
    pallas_call x2, Pallas kernels, exchange(): pl.pallas_call(exchange_kernel, in_specs=[vmem] * 4, out_specs=[vmem] * 2...  62.8 us
    pallas_call x2, Pallas kernels, backward(): pl.pallas_call(lambda *refs: backward_kernel(nb, *refs), grid=(blocks //...  58.6 us
    pallas_call x1, Pallas kernels, own_ray_sums(): pl.pallas_call(ray_sum_kernel, out_shape=jax.ShapeDtypeStruct(shape, jnp....  30.7 us

profile of v5, /device:TPU:0, one launch (start us, length us, event | category | flops | bytes accessed | tf_op | source)
XLA Modules:
  0.0 239.2 jit_solution(9925105976498644310)
XLA Ops:
  0.6 0.7 fusion.37
  1.3 0.6 broadcast_in_dim.129.k_ref
  1.9 0.8 fusion.39
  2.7 0.1 fusion.33
  2.8 0.1 fusion.14
  2.8 0.1 fusion.15
  3.0 0.6 pad_maximum_fusion.1.s_ref
  3.6 0.6 pad_maximum_fusion.c_ref
  4.2 30.7 %raysum.1 = f32[2,8,128]{2,1,0:T(8,128)} custom-call(f32[2,8,128]{2,1,0:T(8,128)} %pad_maximum_fusion.c_ref, f32[2,8,128]{2,1,0:T(8,128)} %pad_maximum_fusion.1.s_ref, f32[2,8,128]{2,1,0:T(8,128)} %broadcast_in_dim.129.k_ref), custom_call_target="tpu_custom_call" | custom-call | tf_op jit(solution)/shard_map/raysum/pallas_call | solution.py:414
  34.9 0.7 copy.28
  35.6 0.1 max.23
  35.7 0.1 copy.24
  35.8 0.1 max.21
  35.8 0.1 copy.22
  35.9 0.7 copy.23.rs_ref
  36.6 0.7 copy.25.rs_ref
  37.3 1.0 fusion.38
  38.3 0.6 reshape.624.mine_ref
  38.9 0.6 reshape.619.mine_ref
  39.5 1.5 fusion.5
  41.0 1.0 add_select_fusion
  42.1 0.1 copy.20
  42.1 0.4 fusion.2
  42.5 0.7 reshape.628.refs_2_
  43.2 0.1 copy.19
  43.3 0.4 fusion
  43.7 0.7 reshape.627.refs_2_
  44.4 0.2 broadcast_in_dim.131
  44.5 0.8 convert_element_type.53.on_ref
  45.3 0.2 broadcast_in_dim.112
  45.5 0.8 convert_element_type.50.on_ref
  46.3 35.4 %forward.2 = f32[1536,128]{1,0:T(8,128)} custom-call(s32[128,8]{1,0:T(8,128)} %get-tuple-element.17.refs_0_, f32[128,8]{1,0:T(8,128)} %get-tuple-element.16.refs_1_, s32[192]{0:T(256)} %reshape.628.refs_2_, s32[8,16]{1,0:T(8,128)} %constant.207.clone.refs_3_, f32[128,8,1024]{2,1,0:T(8,128)} %refs_4_.3, f32[8,1024]{1,0:T(8,128)} %constant.208.clone.refs_5_), custom_call_target="tpu_custom_call" | custom-call | tf_op jit(solution)/shard_map/forward/pallas_call | solution.py:350
  81.7 31.5 %exchange.2 = (f32[4,2,4,48,128]{4,3,2,1,0:T(8,128)}, f32[48,128]{1,0:T(8,128)}) custom-call(f32[4,2,4,48,128]{4,3,2,1,0:T(8,128)} %bitcast.16, f32[48,128]{1,0:T(8,128)} %reshape.619.mine_ref, f32[48,128]{1,0:T(8,128)} %convert_element_type.50.on_ref, f32[48,128]{1,0:T(8,128)} %copy.23.rs_ref), custom_call_target="tpu_custom_call" | custom-call | tf_op jit(solution)/shard_map/exchange/pallas_call | solution.py:324
  113.2 29.2 %backward.2.refs_4_ = f32[128,8,1024]{2,1,0:T(8,128)} custom-call(s32[128,8]{1,0:T(8,128)} %get-tuple-element.17.refs_0_, f32[128,8]{1,0:T(8,128)} %get-tuple-element.16.refs_1_, s32[192]{0:T(256)} %reshape.628.refs_2_, s32[8,16]{1,0:T(8,128)} %constant.207.clone.refs_3_, f32[128,8,1024]{2,1,0:T(8,128)} %refs_4_.3, f32[8,1024]{1,0:T(8,128)} %constant.208.clone.refs_5_, ...), custom_call_target="tpu_custom_call" | custom-call | tf_op jit(solution)/shard_map/backward/pallas_call | solution.py:372
  142.4 35.5 %forward.3 = f32[1536,128]{1,0:T(8,128)} custom-call(s32[128,8]{1,0:T(8,128)} %get-tuple-element.24.refs_0_, f32[128,8]{1,0:T(8,128)} %get-tuple-element.25.refs_1_, s32[192]{0:T(256)} %reshape.627.refs_2_, s32[8,16]{1,0:T(8,128)} %constant.211.clone.refs_3_, f32[128,8,1024]{2,1,0:T(8,128)} %backward.2.refs_4_, f32[8,1024]{1,0:T(8,128)} %constant.212.clone.refs_5_), custom_call_target="tpu_custom_call" | custom-call | tf_op jit(solution)/shard_map/forward/pallas_call | solution.py:350
  178.0 31.2 %exchange.3 = (f32[4,2,4,48,128]{4,3,2,1,0:T(8,128)}, f32[48,128]{1,0:T(8,128)}) custom-call(f32[4,2,4,48,128]{4,3,2,1,0:T(8,128)} %bitcast.17, f32[48,128]{1,0:T(8,128)} %reshape.624.mine_ref, f32[48,128]{1,0:T(8,128)} %convert_element_type.53.on_ref, f32[48,128]{1,0:T(8,128)} %copy.25.rs_ref), custom_call_target="tpu_custom_call" | custom-call | tf_op jit(solution)/shard_map/exchange/pallas_call | solution.py:324
  209.2 0.0 copy-start
  209.2 29.4 %backward.3 = f32[128,8,1024]{2,1,0:T(8,128)} custom-call(s32[128,8]{1,0:T(8,128)} %get-tuple-element.24.refs_0_, f32[128,8]{1,0:T(8,128)} %get-tuple-element.25.refs_1_, s32[192]{0:T(256)} %reshape.627.refs_2_, s32[8,16]{1,0:T(8,128)} %constant.211.clone.refs_3_, f32[128,8,1024]{2,1,0:T(8,128)} %backward.2.refs_4_, f32[8,1024]{1,0:T(8,128)} %constant.212.clone.refs_5_, ...), custom_call_target="tpu_custom_call" | custom-call | tf_op jit(solution)/shard_map/backward/pallas_call | solution.py:372
  238.6 0.0 copy-done
  238.6 0.6 broadcast_in_dim_reshape.3
  (11 shorter events, 0.2 us)
Async XLA Ops:
  209.2 29.4 %copy-start = (f32[48,128]{1,0:T(8,128)S(1)}, f32[48,128]{1,0:T(8,128)}, u32[]{:S(2)}) copy-start(f32[48,128]{1,0:T(8,128)} %get-tuple-element.7) | copy-start | bytes 73732
